TPU v7x, 512 devices: a whole 4x8x8 slice. The times are simulated.
512 devices in a mesh: req: 64 (over x, z, core), tp: 8 (over y).
Axes of the slice: x: 4, y: 8, z: 8, core: 2. Of those that a mesh axis runs over, the one named last changes fastest.
Arguments:
- queries: bfloat16 [4, 512, 1024], P(None, 'req', 'tp'), may hold values from -6 to 6
- new_kv: bfloat16 [4, 512, 2, 1024], P(None, 'req', None, 'tp'), may hold values from -4 to 4
- residual: bfloat16 [4, 512, 2048], P(None, 'req'), may hold values from -1.1953125 to 1.1953125
- home_cache: bfloat16 [256, 128, 2, 1024], P('req', None, None, 'tp'), may hold values from -6 to 6
- prompt_cache: bfloat16 [256, 128, 2, 1024], P('req', None, None, 'tp'), may hold values from -6 to 6
- home_table: int32 [512, 4], P('req'), may hold values from 0 to 3
- home_len: int32 [512], P('req'), may hold values from 1 to 512, as said below
- parents: int32 [4, 512], P(None, 'req'), may hold values from 0 to 7
- prompt_place: int32 [64], P('req'), may hold values from 0 to 63, as said below
- owned_request: int32 [64], P('req'), may hold values from 0 to 63, as said below
- prompt_len: int32 [64], P('req'), may hold values from 1 to 512, as said below
- out_weight: bfloat16 [1024, 2048], P('tp'), may hold values from -0.1875 to 0.1875
- norm_gain: bfloat16 [2048], replicated, may hold values from 0.099609375 to 1.8984375
- qkv_weight: bfloat16 [2048, 3, 1024], P(None, None, 'tp'), may hold values from -0.03125 to 0.03125
Outputs:
- next_qkv: bfloat16 [4, 512, 3, 1024], P(None, 'req', None, 'tp')
- new_residual: bfloat16 [4, 512, 2048], P(None, 'req')
Inputs may be any that keep to these rules, and one draw needn't show every extreme that they name: `home_len`: some beam has all 512 tokens. `prompt_len`: some prompt has all 512 tokens. `prompt_place`: A permutation. Slot j lies on device j. The 1 request of one device have their prompts on 1 different devices, each device holds prompts of 1 request of different devices, and a request's position among its device's requests equals its slot's position j % 1. `owned_request`: the inverse permutation of prompt_place.
All inputs are finite; a program needn't handle non-finite values.
Results may differ from a plain program's by a relative error of at most 0.013.
Values may be sent and summed in bfloat16 or wider, within the bound.
No kernel may reach another device: no remote copies, remote signals or barrier semaphores. Data moves between devices by JAX's collectives and lax.ppermute only.
A program may use at most 64 MiB of HBM per device.

v0:
```python
import math

import jax
import jax.numpy as jnp
from jax import lax
from jax.sharding import PartitionSpec as P

HEAD_DIM = 64
BEAMS = 8


NEG_FILL = -1e30
NORM_EPS = 1e-05


def shards(
    queries,
    new_kv,
    residual,
    home_cache,
    prompt_cache,
    home_table,
    home_len,
    parents,
    prompt_place,
    owned_request,
    prompt_len,
    out_weight,
    norm_gain,
    qkv_weight,
):
    step_count, row_count, lane_count = queries.shape
    head_count = lane_count // HEAD_DIM
    request_count = row_count // BEAMS
    block_count = home_table.shape[1]
    block_size = home_cache.shape[1]
    prompt_tokens = prompt_cache.shape[0] * block_size // request_count
    home_tokens = block_count * block_size
    req_size = lax.axis_size("req")
    score_scale = 1.0 / math.sqrt(HEAD_DIM)
    request_base = jnp.arange(row_count, dtype=jnp.int32) // BEAMS * BEAMS
    first_parent = request_base + parents[0]
    tables = home_table[first_parent]
    lengths = home_len[first_parent]
    window = jnp.zeros((row_count, step_count, 2, lane_count), jnp.bfloat16)
    prompt_heads = prompt_cache.reshape(request_count, prompt_tokens, 2, head_count, HEAD_DIM)
    prompt_pos = jnp.arange(prompt_tokens, dtype=jnp.int32)
    home_pos = jnp.arange(home_tokens, dtype=jnp.int32)
    window_pos = jnp.arange(step_count, dtype=jnp.int32)
    gain_row = norm_gain.astype(jnp.float32)
    weight_flat = qkv_weight.reshape(qkv_weight.shape[0], 3 * lane_count)
    qkv_list = []
    residual_list = []
    for step_index in range(step_count):
        if step_index > 0:
            window = window.at[:, step_index - 1].set(new_kv[step_index - 1])
            chosen = request_base + parents[step_index]
            window = window[chosen]
            tables = tables[chosen]
            lengths = lengths[chosen]
        query_block = queries[step_index : step_index + 1]
        route_block_steps = query_block.shape[0]
        all_queries = lax.all_gather(query_block, "req", axis=1, tiled=True)
        route_query_held = all_queries.reshape(
            route_block_steps, req_size * request_count, BEAMS, head_count, HEAD_DIM
        )[:, owned_request]
        prompt_block_steps = route_query_held.shape[0]
        scores = (
            jnp.einsum(
                "krbhd,rthd->krbht",
                route_query_held,
                prompt_heads[:, :, 0],
                preferred_element_type=jnp.float32,
            )
            * score_scale
        )
        scores = jnp.where(
            prompt_pos[None, None, None, None, :] < prompt_len[None, :, None, None, None],
            scores,
            NEG_FILL,
        )
        row_top = jnp.max(scores, axis=-1)
        weights = jnp.exp(scores - row_top[..., None]).astype(jnp.bfloat16)
        weight_sum = jnp.sum(weights.astype(jnp.float32), axis=-1)
        numerator = jnp.einsum(
            "krbht,rthd->krbhd", weights, prompt_heads[:, :, 1], preferred_element_type=jnp.float32
        )
        held_numer = numerator.reshape(prompt_block_steps, row_count, lane_count)
        held_top = row_top.reshape(prompt_block_steps, row_count, head_count)
        held_sum = weight_sum.reshape(prompt_block_steps, row_count, head_count)
        all_numer = lax.all_gather(held_numer, "req", axis=1, tiled=True)
        all_top = lax.all_gather(held_top, "req", axis=1, tiled=True)
        all_sum_rows = lax.all_gather(held_sum, "req", axis=1, tiled=True)
        route_prompt_numer = all_numer.reshape(
            route_block_steps, req_size * request_count, BEAMS, lane_count
        )[:, prompt_place].reshape(route_block_steps, row_count, lane_count)
        route_prompt_top = all_top.reshape(
            route_block_steps, req_size * request_count, BEAMS, head_count
        )[:, prompt_place].reshape(route_block_steps, row_count, head_count)
        route_prompt_sum = all_sum_rows.reshape(
            route_block_steps, req_size * request_count, BEAMS, head_count
        )[:, prompt_place].reshape(route_block_steps, row_count, head_count)
        attend_prompt_numer = route_prompt_numer[0]
        attend_prompt_top = route_prompt_top[0]
        attend_prompt_sum = route_prompt_sum[0]
        query_heads = queries[step_index].reshape(row_count, head_count, HEAD_DIM)
        gathered = home_cache[tables].reshape(row_count, home_tokens, 2, head_count, HEAD_DIM)
        window_heads = window.reshape(row_count, step_count, 2, head_count, HEAD_DIM)
        own_heads = new_kv[step_index].reshape(row_count, 2, head_count, HEAD_DIM)
        home_scores = (
            jnp.einsum(
                "bhd,bthd->bht", query_heads, gathered[:, :, 0], preferred_element_type=jnp.float32
            )
            * score_scale
        )
        home_scores = jnp.where(
            home_pos[None, None, :] < lengths[:, None, None], home_scores, NEG_FILL
        )
        window_scores = (
            jnp.einsum(
                "bhd,bthd->bht",
                query_heads,
                window_heads[:, :, 0],
                preferred_element_type=jnp.float32,
            )
            * score_scale
        )
        window_scores = jnp.where(window_pos < step_index, window_scores, NEG_FILL)
        own_scores = (
            jnp.einsum(
                "bhd,bhd->bh", query_heads, own_heads[:, 0], preferred_element_type=jnp.float32
            )
            * score_scale
        )
        home_top = jnp.maximum(
            jnp.maximum(jnp.max(home_scores, axis=-1), jnp.max(window_scores, axis=-1)), own_scores
        )
        home_weights = jnp.exp(home_scores - home_top[..., None]).astype(jnp.bfloat16)
        window_weights = jnp.exp(window_scores - home_top[..., None]).astype(jnp.bfloat16)
        own_weights = jnp.exp(own_scores - home_top).astype(jnp.bfloat16)
        home_sum = (
            jnp.sum(home_weights.astype(jnp.float32), axis=-1)
            + jnp.sum(window_weights.astype(jnp.float32), axis=-1)
            + own_weights.astype(jnp.float32)
        )
        home_numer = jnp.einsum(
            "bht,bthd->bhd", home_weights, gathered[:, :, 1], preferred_element_type=jnp.float32
        )
        home_numer = home_numer + jnp.einsum(
            "bht,bthd->bhd",
            window_weights,
            window_heads[:, :, 1],
            preferred_element_type=jnp.float32,
        )
        home_numer = home_numer + own_weights.astype(jnp.float32)[..., None] * own_heads[
            :, 1
        ].astype(jnp.float32)
        attend_prompt_numer = attend_prompt_numer.reshape(row_count, head_count, HEAD_DIM)
        joint_top = jnp.maximum(home_top, attend_prompt_top)
        home_factor = jnp.exp(home_top - joint_top)
        prompt_factor = jnp.exp(attend_prompt_top - joint_top)
        joint_sum = home_sum * home_factor + attend_prompt_sum * prompt_factor
        joint_numer = (
            home_numer * home_factor[..., None] + attend_prompt_numer * prompt_factor[..., None]
        )
        attended = (
            (joint_numer / joint_sum[..., None]).astype(jnp.bfloat16).reshape(row_count, lane_count)
        )
        attended_block = attended[None]
        residual_block = residual[step_index : step_index + 1]
        block_steps = attended_block.shape[0]
        flat_rows = block_steps * row_count
        attended_flat = attended_block.reshape(flat_rows, lane_count)
        residual_flat = residual_block.reshape(flat_rows, residual_block.shape[-1])
        projected = jnp.dot(attended_flat, out_weight, preferred_element_type=jnp.float32)
        head_total = lax.psum(projected, "tp")
        mixed_rows = residual_flat.astype(jnp.float32) + head_total
        mean_square = jnp.mean(mixed_rows * mixed_rows, axis=-1, keepdims=True)
        normed = (mixed_rows * lax.rsqrt(mean_square + NORM_EPS) * gain_row).astype(jnp.bfloat16)
        residual_out = mixed_rows.astype(jnp.bfloat16)
        next_rows = jnp.dot(normed, weight_flat, preferred_element_type=jnp.float32).astype(
            jnp.bfloat16
        )
        qkv_step = next_rows.reshape(block_steps, row_count, 3, lane_count)
        residual_step = residual_out.reshape(block_steps, row_count, residual_out.shape[-1])
        qkv_list.append(qkv_step[0])
        residual_list.append(residual_step[0])
    return (jnp.stack(qkv_list), jnp.stack(residual_list))


def solution(mesh):
    placed = (
        P(None, "req", "tp"),
        P(None, "req", None, "tp"),
        P(None, "req", None),
        P("req", None, None, "tp"),
        P("req", None, None, "tp"),
        P("req", None),
        P("req"),
        P(None, "req"),
        P("req"),
        P("req"),
        P("req"),
        P("tp", None),
        P(),
        P(None, None, "tp"),
    )
    return jax.shard_map(
        shards,
        mesh=mesh,
        in_specs=placed,
        out_specs=(P(None, "req", None, "tp"), P(None, "req", None)),
        check_vma=False,
    )
```

profile of v0, /device:TPU:6, one launch (start us, length us, event | category | flops | bytes accessed | tf_op | source)
XLA Modules:
  0.0 910.0 jit_solution(6705653716037907314)
XLA Ops:
  12.4 6.4 gather_fusion.9
  18.8 2.8 copy.172
  21.5 3.1 reshape.675
  24.7 1.4 slice_bitcast_fusion.3
  30.7 1.9 fusion.22
  33.4 1.3 convert_reduce_fusion.3
  34.7 1.2 convert_reduce_fusion.9
  35.9 55.4 %all_gather.56 = bf16[1,512,128]{2,1,0:T(8,128)(2,1)S(1)} all-gather(bf16[1,8,128]{2,1,0:T(8,128)(2,1)S(1)} %get-tuple-element.276), channel_id=1, replica_groups=mesh['req'=64,'tp'=8] {'req'}, dimensions={1}, use_global_device_ids=true | all-gather | bytes 133120 | tf_op jit(solution)/shard_map/all_gather | solution.py:63
  92.7 47.7 %all_gather.60 = bf16[1,512,128]{2,1,0:T(8,128)(2,1)S(1)} all-gather(bf16[1,8,128]{2,1,0:T(8,128)(2,1)S(1)} %get-tuple-element.279), channel_id=1, replica_groups=mesh['req'=64,'tp'=8] {'req'}, dimensions={1}, use_global_device_ids=true | all-gather | bytes 133120 | tf_op jit(solution)/shard_map/all_gather | solution.py:63
  144.3 5.5 gather_fusion.13
  149.8 2.8 copy.181
  152.6 3.1 reshape.687
  155.7 1.4 slice_bitcast_fusion.1
  158.5 1.9 fusion.18
  161.1 1.3 convert_reduce_fusion.1
  162.4 1.2 convert_reduce_fusion.8
  167.1 5.4 gather_fusion.5
  172.5 2.8 copy.163
  175.3 3.1 reshape.663
  178.4 1.2 slice_bitcast_fusion.5
  181.0 1.3 convert_reduce_fusion.5
  182.2 1.2 convert_reduce_fusion.10
  183.5 48.8 %all_gather.52 = bf16[1,512,128]{2,1,0:T(8,128)(2,1)S(1)} all-gather(bf16[1,8,128]{2,1,0:T(8,128)(2,1)S(1)} %get-tuple-element.277), channel_id=1, replica_groups=mesh['req'=64,'tp'=8] {'req'}, dimensions={1}, use_global_device_ids=true | all-gather | bytes 133120 | tf_op jit(solution)/shard_map/all_gather | solution.py:63
  232.3 47.2 %all_gather.48 = bf16[1,512,128]{2,1,0:T(8,128)(2,1)S(1)} all-gather(bf16[1,8,128]{2,1,0:T(8,128)(2,1)S(1)} %get-tuple-element.278), channel_id=1, replica_groups=mesh['req'=64,'tp'=8] {'req'}, dimensions={1}, use_global_device_ids=true | all-gather | bytes 133120 | tf_op jit(solution)/shard_map/all_gather | solution.py:63
  281.2 0.9 fusion.154
  282.7 0.9 fusion.153
  284.0 43.0 %all-gather.13 = f32[64,8,2]{1,2,0:T(2,128)S(1)} all-gather(f32[1,8,2]{1,2,0:T(2,128)} %bitcast.533), channel_id=7, replica_groups=mesh['req'=64,'tp'=8] {'req'}, dimensions={0}, use_global_device_ids=true | all-gather | bytes 4160 | tf_op jit(solution)/shard_map/all_gather | solution.py:93
  327.0 41.3 %all-gather.12 = f32[64,8,2]{1,2,0:T(2,128)S(1)} all-gather(f32[1,8,2]{1,2,0:T(2,128)S(1)} %bitcast.517), channel_id=6, replica_groups=mesh['req'=64,'tp'=8] {'req'}, dimensions={0}, use_global_device_ids=true | all-gather | bytes 4160 | tf_op jit(solution)/shard_map/all_gather | solution.py:92
  370.9 43.2 %all_gather.58 = f32[1,512,128]{2,1,0:T(8,128)S(1)} all-gather(f32[1,8,128]{2,1,0:T(8,128)S(1)} %reshape.683), channel_id=1, replica_groups=mesh['req'=64,'tp'=8] {'req'}, dimensions={1}, use_global_device_ids=true | all-gather | bytes 266240 | tf_op jit(solution)/shard_map/all_gather | solution.py:91
  414.2 1.4 fusion.20
  416.7 41.3 %all-gather.15 = f32[64,8,2]{1,2,0:T(2,128)S(1)} all-gather(f32[1,8,2]{1,2,0:T(2,128)} %bitcast.534), channel_id=9, replica_groups=mesh['req'=64,'tp'=8] {'req'}, dimensions={0}, use_global_device_ids=true | all-gather | bytes 4160 | tf_op jit(solution)/shard_map/all_gather | solution.py:93
  458.0 42.8 %all-gather.14 = f32[64,8,2]{1,2,0:T(2,128)S(1)} all-gather(f32[1,8,2]{1,2,0:T(2,128)} %bitcast.518), channel_id=8, replica_groups=mesh['req'=64,'tp'=8] {'req'}, dimensions={0}, use_global_device_ids=true | all-gather | bytes 4160 | tf_op jit(solution)/shard_map/all_gather | solution.py:92
  503.4 41.7 %all_gather.62 = f32[1,512,128]{2,1,0:T(8,128)S(1)} all-gather(f32[1,8,128]{2,1,0:T(8,128)S(1)} %reshape.695), channel_id=1, replica_groups=mesh['req'=64,'tp'=8] {'req'}, dimensions={1}, use_global_device_ids=true | all-gather | bytes 266240 | tf_op jit(solution)/shard_map/all_gather | solution.py:91
  547.9 42.8 %all-gather.11 = f32[64,8,2]{1,2,0:T(2,128)S(1)} all-gather(f32[1,8,2]{1,2,0:T(2,128)S(1)} %bitcast.535), channel_id=5, replica_groups=mesh['req'=64,'tp'=8] {'req'}, dimensions={0}, use_global_device_ids=true | all-gather | bytes 4160 | tf_op jit(solution)/shard_map/all_gather | solution.py:93
  590.7 41.3 %all-gather.10 = f32[64,8,2]{1,2,0:T(2,128)S(1)} all-gather(f32[1,8,2]{1,2,0:T(2,128)S(1)} %bitcast.519), channel_id=4, replica_groups=mesh['req'=64,'tp'=8] {'req'}, dimensions={0}, use_global_device_ids=true | all-gather | bytes 4160 | tf_op jit(solution)/shard_map/all_gather | solution.py:92
  632.6 43.5 %all_gather.54 = f32[1,512,128]{2,1,0:T(8,128)S(1)} all-gather(f32[1,8,128]{2,1,0:T(8,128)S(1)} %reshape.671), channel_id=1, replica_groups=mesh['req'=64,'tp'=8] {'req'}, dimensions={1}, use_global_device_ids=true | all-gather | bytes 266240 | tf_op jit(solution)/shard_map/all_gather | solution.py:91
  678.1 5.4 gather_fusion.2
  683.5 2.8 copy.151
  686.3 3.1 reshape.649
  689.4 1.5 slice_bitcast_fusion.7
  691.2 1.9 fusion.30
  693.4 41.3 %all-gather.9 = f32[64,8,2]{1,2,0:T(2,128)S(1)} all-gather(f32[1,8,2]{1,2,0:T(2,128)S(1)} %bitcast.532), channel_id=3, replica_groups=mesh['req'=64,'tp'=8] {'req'}, dimensions={0}, use_global_device_ids=true | all-gather | bytes 4160 | tf_op jit(solution)/shard_map/all_gather | solution.py:93
  734.7 42.8 %all-gather.8 = f32[64,8,2]{1,2,0:T(2,128)S(1)} all-gather(f32[1,8,2]{1,2,0:T(2,128)S(1)} %bitcast.516), channel_id=2, replica_groups=mesh['req'=64,'tp'=8] {'req'}, dimensions={0}, use_global_device_ids=true | all-gather | bytes 4160 | tf_op jit(solution)/shard_map/all_gather | solution.py:92
  778.3 41.7 %all_gather.50 = f32[1,512,128]{2,1,0:T(8,128)S(1)} all-gather(f32[1,8,128]{2,1,0:T(8,128)S(1)} %reshape.658), channel_id=1, replica_groups=mesh['req'=64,'tp'=8] {'req'}, dimensions={1}, use_global_device_ids=true | all-gather | bytes 266240 | tf_op jit(solution)/shard_map/all_gather | solution.py:91
  821.8 1.7 copy.160
  823.5 74.0 %all-reduce.4.cloned.1.call-done = (f32[8,2048]{1,0:T(8,128)}, f32[8,2048]{1,0:T(8,128)}, f32[8,2048]{1,0:T(8,128)}, f32[8,2048]{1,0:T(8,128)}) async-done(((f32[8,2048]{1,0:T(8,128)}, f32[8,2048]{1,0:T(8,128)}, f32[8,2048]{1,0:T(8,128)}, f32[8,2048]{1,0:T(8,128)}), (f32[8,2048]{1,0:T(8,128)}, f32[8,2048]{1,0:T(8,128)}, f32[8,2048]{1,0:T(8,128)}, f32[8,2048]{1,0:T(8,128)})) %all-reduce.4.cloned.1.call-update) | async-done | bytes 262160 | tf_op jit(solution)/shard_map/psum | solution.py:176
  897.5 1.1 multiply_reduce_fusion.3
  898.7 1.3 fusion.12
  (260 shorter events, 41.1 us)
Async XLA Ops:
  7.2 539.1 %copy-start = (bf16[128,2048]{1,0:T(8,128)(2,1)S(1)}, bf16[128,2048]{1,0:T(8,128)(2,1)}, u32[]{:S(2)}) copy-start(bf16[128,2048]{1,0:T(8,128)(2,1)} %param.31) | copy-start | bytes 1572868
  7.2 890.3 %all-reduce.4.cloned.1.call-start = ((), (), s32[]{:S(2)}) async-start(), calls=%async_computation | async-start | bytes 524288 | tf_op jit(solution)/shard_map/psum | solution.py:176
  24.6 1.5 copy-start.1
  24.6 3.5 copy-start.12
  26.8 113.8 %copy-start.8 = (bf16[4,128,2,128]{3,2,1,0:T(2,128)(2,1)S(1)}, bf16[4,128,2,128]{3,2,1,0:T(2,128)(2,1)}, u32[]{:S(2)}) copy-start(bf16[4,128,2,128]{3,2,1,0:T(2,128)(2,1)} %param.24) | copy-start | bytes 786436
  30.7 113.6 %copy-start.2 = (bf16[4,128,2,128]{3,2,1,0:T(2,128)(2,1)S(1)}, bf16[4,128,2,128]{3,2,1,0:T(2,128)(2,1)}, u32[]{:S(2)}) copy-start(bf16[4,128,2,128]{3,2,1,0:T(2,128)(2,1)} %param.23) | copy-start | bytes 786436
  33.0 116.8 %copy-start.13 = (bf16[8,2,2,64]{3,2,1,0:T(2,128)(2,1)}, bf16[8,2,2,64]{3,2,1,0:T(2,128)(2,1)S(1)}, u32[]{:S(2)}) copy-start(bf16[8,2,2,64]{3,2,1,0:T(2,128)(2,1)S(1)} %reshape_squeeze.29) | copy-start | bytes 12292
  33.2 108.4 %copy-start.29 = (f32[8,2]{0,1:T(2,128)}, f32[8,2]{0,1:T(2,128)S(1)}, u32[]{:S(2)}) copy-start(f32[8,2]{0,1:T(2,128)S(1)} %copy.224) | copy-start | bytes 196
  33.4 116.5 %copy-start.19 = (f32[8,2]{0,1:T(2,128)}, f32[8,2]{0,1:T(2,128)S(1)}, u32[]{:S(2)}) copy-start(f32[8,2]{0,1:T(2,128)S(1)} %maximum_maximum_fusion.1) | copy-start | bytes 196
  141.5 22.1 %copy-start.33 = (pred[512]{0:T(512)(128)(4,1)}, pred[512]{0:T(512)(128)(4,1)S(1)}, u32[]{:S(2)}) copy-start(pred[512]{0:T(512)(128)(4,1)S(1)} %iota_compare_fusion.4) | copy-start | bytes 1540
  160.7 6.4 copy-start.14
  160.9 11.6 %copy-start.30 = (f32[8,2]{0,1:T(2,128)}, f32[8,2]{0,1:T(2,128)S(1)}, u32[]{:S(2)}) copy-start(f32[8,2]{0,1:T(2,128)S(1)} %copy.239) | copy-start | bytes 196
  161.1 6.0 copy-start.20
  163.8 3.3 copy-start.18
  179.6 234.6 %copy-start.3 = (bf16[8,512,2,64]{1,0,3,2:T(8,128)(2,1)S(1)}, bf16[8,512,2,64]{1,0,3,2:T(8,128)(2,1)}, u32[]{:S(2)}) copy-start(bf16[8,512,2,64]{1,0,3,2:T(8,128)(2,1)} %get-tuple-element.246) | copy-start | bytes 3145732
  180.6 1.7 copy-start.16
  180.8 1.5 copy-start.31
  180.9 1.3 copy-start.21
  183.5 361.8 %copy-start.4 = (bf16[8,512,2,64]{1,0,3,2:T(8,128)(2,1)S(1)}, bf16[8,512,2,64]{1,0,3,2:T(8,128)(2,1)}, u32[]{:S(2)}) copy-start(bf16[8,512,2,64]{1,0,3,2:T(8,128)(2,1)} %get-tuple-element.248) | copy-start | bytes 3145732
  280.5 135.2 %copy-start.26 = (bf16[8,4,2,64]{3,2,1,0:T(2,128)(2,1)S(1)}, bf16[8,4,2,64]{3,2,1,0:T(2,128)(2,1)}, u32[]{:S(2)}) copy-start(bf16[8,4,2,64]{3,2,1,0:T(2,128)(2,1)} %get-tuple-element.265) | copy-start | bytes 24580
  280.5 264.7 %copy-start.23 = (bf16[8,2,512,1]{2,0,1,3:T(8,128)(2,1)S(1)}, bf16[8,2,512,1]{2,0,1,3:T(8,128)(2,1)}, u32[]{:S(2)}) copy-start(bf16[8,2,512,1]{2,0,1,3:T(8,128)(2,1)} %get-tuple-element.260) | copy-start | bytes 49156
  282.3 263.7 %copy-start.28 = (bf16[8,4,2,64]{3,2,1,0:T(2,128)(2,1)S(1)}, bf16[8,4,2,64]{3,2,1,0:T(2,128)(2,1)}, u32[]{:S(2)}) copy-start(bf16[8,4,2,64]{3,2,1,0:T(2,128)(2,1)} %get-tuple-element.267) | copy-start | bytes 24580
  282.3 263.8 %copy-start.15 = (bf16[8,2,2,64]{3,2,1,0:T(2,128)(2,1)S(1)}, bf16[8,2,2,64]{3,2,1,0:T(2,128)(2,1)}, u32[]{:S(2)}) copy-start(bf16[8,2,2,64]{3,2,1,0:T(2,128)(2,1)} %copy-done.14) | copy-start | bytes 12292
  414.2 217.8 %copy-start.22 = (f32[8,2]{0,1:T(2,128)S(1)}, f32[8,2]{0,1:T(2,128)}, u32[]{:S(2)}) copy-start(f32[8,2]{0,1:T(2,128)} %copy-done.21) | copy-start | bytes 196
  414.2 217.8 %copy-start.32 = (f32[8,2]{0,1:T(2,128)S(1)}, f32[8,2]{0,1:T(2,128)}, u32[]{:S(2)}) copy-start(f32[8,2]{0,1:T(2,128)} %copy-done.31) | copy-start | bytes 196
  414.2 217.8 %copy-start.36 = (f32[8,2]{0,1:T(2,128)S(1)}, f32[8,2]{0,1:T(2,128)}, u32[]{:S(2)}) copy-start(f32[8,2]{0,1:T(2,128)} %get-tuple-element.261) | copy-start | bytes 196
  414.2 217.8 %copy-start.38 = (f32[8,2]{0,1:T(2,128)S(1)}, f32[8,2]{0,1:T(2,128)}, u32[]{:S(2)}) copy-start(f32[8,2]{0,1:T(2,128)} %get-tuple-element.238) | copy-start | bytes 196
  414.2 218.1 %copy-start.34 = (bf16[8,2,4]{0,2,1:T(4,128)(2,1)S(1)}, bf16[8,2,4]{0,2,1:T(4,128)(2,1)}, u32[]{:S(2)}) copy-start(bf16[8,2,4]{0,2,1:T(4,128)(2,1)} %get-tuple-element.239) | copy-start | bytes 388
  415.6 260.5 %copy-start.5 = (bf16[8,512,2,64]{1,0,3,2:T(8,128)(2,1)S(1)}, bf16[8,512,2,64]{1,0,3,2:T(8,128)(2,1)}, u32[]{:S(2)}) copy-start(bf16[8,512,2,64]{1,0,3,2:T(8,128)(2,1)} %get-tuple-element.250) | copy-start | bytes 3145732
  415.6 260.5 %copy-start.24 = (bf16[8,2,512,1]{2,0,1,3:T(8,128)(2,1)S(1)}, bf16[8,2,512,1]{2,0,1,3:T(8,128)(2,1)}, u32[]{:S(2)}) copy-start(bf16[8,2,512,1]{2,0,1,3:T(8,128)(2,1)} %get-tuple-element.262) | copy-start | bytes 49156
  545.2 131.5 %copy-start.27 = (bf16[8,4,2,64]{3,2,0,1:T(2,128)(2,1)S(1)}, bf16[8,4,2,64]{3,2,0,1:T(2,128)(2,1)}, u32[]{:S(2)}) copy-start(bf16[8,4,2,64]{3,2,0,1:T(2,128)(2,1)} %get-tuple-element.269) | copy-start | bytes 24580
  545.2 131.7 %copy-start.17 = (bf16[8,2,2,64]{3,2,1,0:T(2,128)(2,1)S(1)}, bf16[8,2,2,64]{3,2,1,0:T(2,128)(2,1)}, u32[]{:S(2)}) copy-start(bf16[8,2,2,64]{3,2,1,0:T(2,128)(2,1)} %copy-done.16) | copy-start | bytes 12292
  545.9 132.0 %copy-start.35 = (s32[8,4,1]{0,1,2:T(4,128)S(1)}, s32[8,4,1]{0,1,2:T(4,128)}, u32[]{:S(2)}) copy-start(s32[8,4,1]{0,1,2:T(4,128)} %get-tuple-element.299) | copy-start | bytes 388
  689.4 1.5 copy-start.25
  690.9 129.1 %copy-start.6 = (bf16[8,512,2,64]{1,0,3,2:T(8,128)(2,1)S(1)}, bf16[8,512,2,64]{1,0,3,2:T(8,128)(2,1)}, u32[]{:S(2)}) copy-start(bf16[8,512,2,64]{1,0,3,2:T(8,128)(2,1)} %get-tuple-element.252) | copy-start | bytes 3145732
  820.7 2.8 copy-start.37
  820.7 76.8 %copy-start.7 = (bf16[4,8,2048]{2,1,0:T(8,128)(2,1)S(1)}, bf16[4,8,2048]{2,1,0:T(8,128)(2,1)}, u32[]{:S(2)}) copy-start(bf16[4,8,2048]{2,1,0:T(8,128)(2,1)} %param.22) | copy-start | bytes 393220
  897.5 2.5 copy-start.11
  897.5 3.1 copy-start.10
  900.0 1.1 copy-start.9
Sparse Core Ops, SparseCore 0:
  821.9 75.5 all-reduce.3
where the time goes:
time: 916 us; the launch traced here: 910 us
  blocking collectives  706 us (77%)
  local copies, waits for them, and re-layouts  74.8 us (8%)
  waiting for transfers between devices  74 us (8%)
  matrix products  21.2 us (2%)
  other arithmetic  17.5 us (2%)
  between operations  16.8 us (2%)
    all_gather x4, blocking collectives, shards(): all_queries = lax.all_gather(query_block, 'req', axis=1, tiled=True)  199 us
    all_gather x4, blocking collectives, shards(): all_numer = lax.all_gather(held_numer, 'req', axis=1, tiled=True)  170 us
    all_gather x4, blocking collectives, shards(): all_sum_rows = lax.all_gather(held_sum, 'req', axis=1, tiled=True)  168 us
    all_gather x4, blocking collectives, shards(): all_top = lax.all_gather(held_top, 'req', axis=1, tiled=True)  168 us
    psum x1, waiting for transfers between devices, shards(): head_total = lax.psum(projected, 'tp')  74 us
    gather x8, local copies, waits for them, and re-layouts, shards(): home_cache[tables].reshape(row_count, home_tokens, 2, head_count, HEAD_DIM)  33.7 us
  transfers between devices with their start and end apart: 1, of which 1 were waited for; matrix products, arithmetic and copies ran while one was open for 0% of the time, Pallas kernels for 0%

commit v1 on v0

v1 whole, which is shorter than its diff:
```python
import math

import jax
import jax.numpy as jnp
from jax import lax
from jax.experimental import pallas as pl
from jax.experimental.pallas import tpu as pltpu
from jax.sharding import PartitionSpec as P

HEAD_DIM = 64
BEAMS = 8

NEG_FILL = -1e30
NORM_EPS = 1e-05
SCORE_SCALE = 1.0 / math.sqrt(HEAD_DIM)
LANES = 2 * HEAD_DIM
STAT_ROWS = 8


def split_heads(rows):
    lane = lax.broadcasted_iota(jnp.int32, rows.shape, 1)
    zero = jnp.zeros_like(rows)
    return jnp.concatenate(
        [jnp.where(lane < HEAD_DIM, rows, zero), jnp.where(lane >= HEAD_DIM, rows, zero)], axis=0
    )


def join_heads(rows):
    half = rows.shape[0] // 2
    lane = lax.broadcasted_iota(jnp.int32, (half, rows.shape[1]), 1)
    return jnp.where(lane < HEAD_DIM, rows[:half], rows[half:])


def dot_rows(left, right):
    return lax.dot_general(
        left, right, (((1,), (1,)), ((), ())), preferred_element_type=jnp.float32
    )


def to_value_rows(weights):
    return pltpu.roll(weights, 1, axis=1).astype(jnp.bfloat16)


def prompt_kernel(owned_ref, live_ref, held_ref, cache_ref, out_ref, query_ref, sem):
    owner = owned_ref[0]
    chips = held_ref.shape[0] // 2
    slot = (owner % 2) * chips + owner // 2
    copy = pltpu.make_async_copy(held_ref.at[slot], query_ref, sem)
    copy.start()
    copy.wait()
    rows = query_ref.shape[0]
    queries = split_heads(query_ref[...])
    cache = cache_ref[...]
    scores = dot_rows(queries, cache) * SCORE_SCALE
    column = lax.broadcasted_iota(jnp.int32, scores.shape, 1)
    valid = jnp.logical_and(column % 2 == 0, column < 2 * live_ref[0])
    scores = jnp.where(valid, scores, NEG_FILL)
    top = jnp.max(scores, axis=1, keepdims=True)
    weights = jnp.exp(scores - top).astype(jnp.bfloat16).astype(jnp.float32)
    total = jnp.sum(weights, axis=1, keepdims=True)
    numer = jnp.dot(to_value_rows(weights), cache, preferred_element_type=jnp.float32)
    mean = join_heads(numer / total).astype(jnp.bfloat16)
    level = top + jnp.log(total)
    high = level.astype(jnp.bfloat16).astype(jnp.float32)
    rest = level - high
    middle = rest.astype(jnp.bfloat16).astype(jnp.float32)
    low = rest - middle
    wide = (2 * rows, LANES)
    lane = lax.broadcasted_iota(jnp.int32, wide, 1)
    row = lax.broadcasted_iota(jnp.int32, wide, 0)
    on_row = lane % HEAD_DIM == row
    first = jnp.sum(
        jnp.where(on_row, jnp.where(lane < HEAD_DIM, high, middle), 0.0), axis=0, keepdims=True
    )
    second = jnp.sum(jnp.where(on_row, low, 0.0), axis=0, keepdims=True)
    stat_row = lax.broadcasted_iota(jnp.int32, (STAT_ROWS, LANES), 0)
    stats = jnp.where(stat_row == 0, first, jnp.where(stat_row == 1, second, 0.0))
    packet = jnp.concatenate([mean.astype(jnp.float32), stats], axis=0).astype(jnp.bfloat16)
    for index in range(out_ref.shape[0]):
        out_ref[index] = packet


def home_kernel(
    place_ref,
    table_ref,
    length_ref,
    parent_ref,
    query_ref,
    home_ref,
    fresh_ref,
    result_ref,
    out_ref,
    root_ref,
    line_ref,
    packet_ref,
    sem,
):
    place = place_ref[0]
    chips = result_ref.shape[0] // 2
    slot = (place % 2) * chips + place // 2
    copy = pltpu.make_async_copy(result_ref.at[slot], packet_ref, sem)
    copy.start()
    step_count = parent_ref.shape[0]
    block_count = table_ref.shape[0]
    rows = query_ref.shape[0]
    block_tokens = home_ref.shape[0] // (2 * block_count)
    unit = (BEAMS, LANES)
    beam_row = lax.broadcasted_iota(jnp.int32, unit, 0)
    lane = lax.broadcasted_iota(jnp.int32, unit, 1)
    is_key = lane % 2 == 0
    half_lane = lane // 2

    def column_of(values):
        built = jnp.full(unit, values[0], jnp.int32)
        for beam in range(1, BEAMS):
            built = jnp.where(beam_row == beam, values[beam], built)
        return built

    counts = []
    fresh_masks = []
    for step in range(step_count):
        roots = []
        for beam in range(BEAMS):
            parent = parent_ref[step, beam]
            root = parent if step == 0 else root_ref[step - 1, parent]
            root_ref[step, beam] = root
            roots.append(root)
            line_ref[step * step_count + step, beam] = beam
            for source in range(step):
                line_ref[step * step_count + source, beam] = line_ref[
                    (step - 1) * step_count + source, parent
                ]
        length = column_of([length_ref[root] for root in roots])
        entries = [
            column_of([table_ref[entry, root] for root in roots]) for entry in range(block_count)
        ]
        pieces = []
        for block in range(block_count):
            limits = [
                jnp.where(entries[entry] == block, length - entry * block_tokens, 0)
                for entry in range(block_count)
            ]
            for part in range(2 * block_tokens // LANES):
                offset = half_lane + part * (LANES // 2)
                count = jnp.zeros(unit, jnp.float32)
                for limit in limits:
                    count = count + jnp.where(offset < limit, 1.0, 0.0)
                pieces.append(jnp.where(is_key, count, 0.0))
        counts.append(jnp.concatenate(pieces, axis=1))
        seen = jnp.zeros(unit, jnp.float32)
        for source in range(step + 1):
            if source == step:
                target = beam_row + source * BEAMS
            else:
                target = (
                    column_of([line_ref[step * step_count + source, beam] for beam in range(BEAMS)])
                    + source * BEAMS
                )
            seen = jnp.where(half_lane == target, 1.0, seen)
        fresh_masks.append(jnp.where(is_key, seen, 0.0))
    count = jnp.concatenate(counts * 2, axis=0)
    fresh_mask = jnp.concatenate(fresh_masks * 2, axis=0)

    queries = split_heads(query_ref[...])
    home = home_ref[...]
    fresh = fresh_ref[...]
    fresh = jnp.concatenate(
        [fresh, jnp.zeros((LANES - fresh.shape[0], LANES), fresh.dtype)], axis=0
    )
    scores = jnp.where(count > 0.0, dot_rows(queries, home) * SCORE_SCALE, NEG_FILL)
    fresh_scores = jnp.where(fresh_mask > 0.0, dot_rows(queries, fresh) * SCORE_SCALE, NEG_FILL)
    top = jnp.maximum(
        jnp.max(scores, axis=1, keepdims=True), jnp.max(fresh_scores, axis=1, keepdims=True)
    )
    weights = jnp.exp(scores - top).astype(jnp.bfloat16).astype(jnp.float32) * count
    weights = weights.astype(jnp.bfloat16).astype(jnp.float32)
    fresh_weights = jnp.exp(fresh_scores - top).astype(jnp.bfloat16).astype(jnp.float32)
    total = jnp.sum(weights, axis=1, keepdims=True) + jnp.sum(fresh_weights, axis=1, keepdims=True)
    numer = jnp.dot(to_value_rows(weights), home, preferred_element_type=jnp.float32)
    numer = numer + jnp.dot(
        to_value_rows(fresh_weights), fresh, preferred_element_type=jnp.float32
    )

    copy.wait()
    packet = packet_ref[...].astype(jnp.float32)
    mean = packet[:rows]
    wide = (2 * rows, LANES)
    wide_lane = lax.broadcasted_iota(jnp.int32, wide, 1)
    wide_row = lax.broadcasted_iota(jnp.int32, wide, 0)
    on_row = wide_lane % HEAD_DIM == wide_row
    low_half = wide_lane < HEAD_DIM
    level = jnp.sum(
        jnp.where(on_row, jnp.broadcast_to(packet[rows : rows + 1], wide), 0.0),
        axis=1,
        keepdims=True,
    ) + jnp.sum(
        jnp.where(
            jnp.logical_and(on_row, low_half),
            jnp.broadcast_to(packet[rows + 1 : rows + 2], wide),
            0.0,
        ),
        axis=1,
        keepdims=True,
    )
    joint_top = jnp.maximum(top, level)
    home_factor = jnp.exp(top - joint_top)
    prompt_factor = jnp.exp(level - joint_top)
    both = jnp.concatenate([mean, mean], axis=0)
    attended = (numer * home_factor + both * prompt_factor) / (
        total * home_factor + prompt_factor
    )
    attended = join_heads(attended).astype(jnp.bfloat16)
    for index in range(out_ref.shape[0]):
        out_ref[index] = attended


def mix_kernel(
    attended_ref, weight_ref, residual_ref, gain_ref, qkv_weight_ref, qkv_ref, residual_out_ref
):
    shard_count = attended_ref.shape[0]
    attended = jnp.concatenate([attended_ref[index] for index in range(shard_count)], axis=1)
    mixed = residual_ref[...].astype(jnp.float32) + jnp.dot(
        attended, weight_ref[...], preferred_element_type=jnp.float32
    )
    residual_out_ref[...] = mixed.astype(jnp.bfloat16)
    mean_square = jnp.mean(mixed * mixed, axis=1, keepdims=True)
    gain = gain_ref[...].astype(jnp.float32)
    normed = (mixed * lax.rsqrt(mean_square + NORM_EPS) * gain).astype(jnp.bfloat16)
    for kind in range(qkv_weight_ref.shape[0]):
        projected = jnp.dot(
            normed, qkv_weight_ref[kind], preferred_element_type=jnp.float32
        ).astype(jnp.bfloat16)
        for step in range(qkv_ref.shape[0]):
            qkv_ref[step, kind] = projected[step * BEAMS : (step + 1) * BEAMS]


VMEM_SPEC = pl.BlockSpec(memory_space=pltpu.VMEM)
SMEM_SPEC = pl.BlockSpec(memory_space=pltpu.SMEM)
ANY_SPEC = pl.BlockSpec(memory_space=pl.ANY)


def shards(
    queries,
    new_kv,
    residual,
    home_cache,
    prompt_cache,
    home_table,
    home_len,
    parents,
    prompt_place,
    owned_request,
    prompt_len,
    out_weight,
    norm_gain,
    qkv_weight,
):
    step_count, row_count, lane_count = queries.shape
    model_width = residual.shape[-1]
    rows = step_count * row_count
    req_size = lax.axis_size("req")
    tp_size = lax.axis_size("tp")
    chips = req_size // 2
    same_core = [[2 * chip + core for chip in range(chips)] for core in range(2)]
    same_chip = [[2 * chip, 2 * chip + 1] for chip in range(chips)]

    def route(slots):
        arrived = lax.all_to_all(slots, "req", 0, 0, axis_index_groups=same_core)
        return lax.all_gather(arrived, "req", axis_index_groups=same_chip, tiled=True)

    whole_weight = lax.all_gather(out_weight, "tp", axis=0, tiled=True)

    query_rows = queries.reshape(rows, lane_count)
    held = route(jnp.broadcast_to(query_rows[None], (chips, rows, lane_count)))
    prompt_rows = prompt_cache.reshape(-1, lane_count)
    packet_rows = rows + STAT_ROWS
    results = pl.pallas_call(
        prompt_kernel,
        out_shape=jax.ShapeDtypeStruct((chips, packet_rows, lane_count), jnp.bfloat16),
        in_specs=[SMEM_SPEC, SMEM_SPEC, ANY_SPEC, VMEM_SPEC],
        out_specs=VMEM_SPEC,
        scratch_shapes=[pltpu.VMEM((rows, lane_count), jnp.bfloat16), pltpu.SemaphoreType.DMA],
        name="prompt_attention",
    )(owned_request, prompt_len, held, prompt_rows)
    returned = route(results)

    home_rows = home_cache.reshape(-1, lane_count)
    fresh_rows = new_kv.reshape(-1, lane_count)
    attended = pl.pallas_call(
        home_kernel,
        out_shape=jax.ShapeDtypeStruct((tp_size, rows, lane_count), jnp.bfloat16),
        in_specs=[SMEM_SPEC] * 4 + [VMEM_SPEC] * 3 + [ANY_SPEC],
        out_specs=VMEM_SPEC,
        scratch_shapes=[
            pltpu.SMEM((step_count, BEAMS), jnp.int32),
            pltpu.SMEM((step_count * step_count, BEAMS), jnp.int32),
            pltpu.VMEM((packet_rows, lane_count), jnp.bfloat16),
            pltpu.SemaphoreType.DMA,
        ],
        name="home_attention",
    )(
        prompt_place,
        home_table.T,
        home_len,
        parents,
        query_rows,
        home_rows,
        fresh_rows,
        returned,
    )
    all_heads = lax.all_to_all(attended, "tp", 0, 0)
    next_qkv, new_residual = pl.pallas_call(
        mix_kernel,
        out_shape=(
            jax.ShapeDtypeStruct((step_count, 3, row_count, lane_count), jnp.bfloat16),
            jax.ShapeDtypeStruct((rows, model_width), jnp.bfloat16),
        ),
        in_specs=[VMEM_SPEC] * 5,
        out_specs=(VMEM_SPEC, VMEM_SPEC),
        compiler_params=pltpu.CompilerParams(vmem_limit_bytes=40 * 1024 * 1024),
        name="mix",
    )(
        all_heads,
        whole_weight,
        residual.reshape(rows, model_width),
        norm_gain.reshape(1, model_width),
        qkv_weight.transpose(1, 0, 2),
    )
    return (
        next_qkv.transpose(0, 2, 1, 3),
        new_residual.reshape(step_count, row_count, model_width),
    )


def solution(mesh):
    placed = (
        P(None, "req", "tp"),
        P(None, "req", None, "tp"),
        P(None, "req", None),
        P("req", None, None, "tp"),
        P("req", None, None, "tp"),
        P("req", None),
        P("req"),
        P(None, "req"),
        P("req"),
        P("req"),
        P("req"),
        P("tp", None),
        P(),
        P(None, None, "tp"),
    )
    return jax.shard_map(
        shards,
        mesh=mesh,
        in_specs=placed,
        out_specs=(P(None, "req", None, "tp"), P(None, "req", None)),
        check_vma=False,
    )
```

time: 916 us -> 90.3 us (0.10)
  the two profiles are of different devices: /device:TPU:6 before, /device:TPU:1 now
where the time goes in v1:
time: 90.3 us; the launch traced here: 89.7 us
  waiting for transfers between devices  26.1 us (29%)
  starting transfers between devices  24.7 us (27%)
  between operations  16 us (18%)
  blocking collectives  11.5 us (13%)
  Pallas kernels  7.64 us (8%)
  local copies, waits for them, and re-layouts  3.64 us (4%)
    all_to_all x2, waiting for transfers between devices, route(): arrived = lax.all_to_all(slots, 'req', 0, 0, axis_index_groups=same_core)  18.2 us
    all_to_all x2, starting transfers between devices, route(): arrived = lax.all_to_all(slots, 'req', 0, 0, axis_index_groups=same_core)  17.8 us
    all_gather x2, blocking collectives, route(): lax.all_gather(arrived, 'req', axis_index_groups=same_chip, tiled=True)  11.5 us
    all_to_all x1, waiting for transfers between devices, shards(): all_heads = lax.all_to_all(attended, 'tp', 0, 0)  7.22 us
    all_to_all x1, starting transfers between devices, shards(): all_heads = lax.all_to_all(attended, 'tp', 0, 0)  6.85 us
    pallas_call x1, Pallas kernels, shards(): pl.pallas_call(prompt_kernel, out_shape=jax.ShapeDtypeStruct((chips, pack...  2.93 us
    pallas_call x1, Pallas kernels, shards(): pl.pallas_call(home_kernel, out_shape=jax.ShapeDtypeStruct((tp_size, rows...  2.85 us
    unnamed x8, local copies, waits for them, and re-layouts  2.2 us
  transfers between devices with their start and end apart: 4, of which 3 were waited for; matrix products, arithmetic and copies ran while one was open for 2% of the time, Pallas kernels for 6%

profile of v1, /device:TPU:1, one launch (start us, length us, event | category | flops | bytes accessed | tf_op | source)
XLA Modules:
  0.0 89.7 jit_solution(2513849795123591775)
XLA Ops:
  7.2 0.0 copy-start.3
  7.2 0.0 copy-start.2
  7.2 0.0 copy-start.1
  7.2 0.0 all-gather.2.cloned.1.call-start
  7.2 0.7 all-gather.2.cloned.1.call-update
  7.9 1.4 %broadcast_in_dim.2 = bf16[32,32,128]{2,1,0:T(8,128)(2,1)} broadcast(bf16[32,128]{1,0:T(8,128)(2,1)} %bitcast.13), dimensions={1,2} | broadcast | bytes 270336 | tf_op jit(solution)/shard_map/broadcast_in_dim | solution.py:274
  9.4 13.7 %all-to-all-start = ((bf16[32,32,128]{2,1,0:T(8,128)(2,1)}), bf16[32,32,128]{2,1,0:T(8,128)(2,1)S(1)}, u32[]{:S(2)}, u32[]{:S(2)}) async-start(bf16[32,32,128]{2,1,0:T(8,128)(2,1)} %broadcast_in_dim.2), calls=%async_computation | async-start | bytes 524288 | tf_op jit(solution)/shard_map/all_to_all | solution.py:268
  24.4 8.4 %all-to-all-done = bf16[32,32,128]{2,1,0:T(8,128)(2,1)S(1)} async-done(((bf16[32,32,128]{2,1,0:T(8,128)(2,1)}), bf16[32,32,128]{2,1,0:T(8,128)(2,1)S(1)}, u32[]{:S(2)}, u32[]{:S(2)}) %all-to-all-start) | async-done | bytes 262176 | tf_op jit(solution)/shard_map/all_to_all | solution.py:268
  32.8 5.7 %all_gather.9.held_ref = bf16[64,32,128]{2,1,0:T(8,128)(2,1)} all-gather(bf16[32,32,128]{2,1,0:T(8,128)(2,1)S(1)} %all-to-all-done), channel_id=1, replica_groups={{0,8},{16,24},{32,40},{48,56},{64,72},{80,88},{96,104},{112,120},{128,1..., dimensions={0}, use_global_device_ids=true | all-gather | bytes 786432 | tf_op jit(solution)/shard_map/all_gather | solution.py:269
  38.4 2.9 %prompt_attention.1 = bf16[32,40,128]{2,1,0:T(8,128)(2,1)} custom-call(s32[1]{0:T(128)S(6)} %copy.17.owned_ref, s32[1]{0:T(128)S(6)} %copy.18.live_ref, bf16[64,32,128]{2,1,0:T(8,128)(2,1)} %all_gather.9.held_ref, bf16[1024,128]{1,0:T(8,128)(2,1)} %bitcast.11), custom_call_target="tpu_custom_call" | custom-call | tf_op jit(solution)/shard_map/prompt_attention/pallas_call | solution.py:277
  41.4 4.1 %all-to-all-start.1 = ((bf16[32,40,128]{2,1,0:T(8,128)(2,1)}), bf16[32,40,128]{2,1,0:T(8,128)(2,1)S(1)}, u32[]{:S(2)}, u32[]{:S(2)}) async-start(bf16[32,40,128]{2,1,0:T(8,128)(2,1)} %prompt_attention.1), calls=%async_computation.1 | async-start | bytes 655360 | tf_op jit(solution)/shard_map/all_to_all | solution.py:268
  46.1 9.8 %all-to-all-done.1 = bf16[32,40,128]{2,1,0:T(8,128)(2,1)S(1)} async-done(((bf16[32,40,128]{2,1,0:T(8,128)(2,1)}), bf16[32,40,128]{2,1,0:T(8,128)(2,1)S(1)}, u32[]{:S(2)}, u32[]{:S(2)}) %all-to-all-start.1) | async-done | bytes 327712 | tf_op jit(solution)/shard_map/all_to_all | solution.py:268
  56.0 5.9 %all_gather.10.result_ref = bf16[64,40,128]{2,1,0:T(8,128)(2,1)} all-gather(bf16[32,40,128]{2,1,0:T(8,128)(2,1)S(1)} %all-to-all-done.1), channel_id=1, replica_groups={{0,8},{16,24},{32,40},{48,56},{64,72},{80,88},{96,104},{112,120},{128,1..., dimensions={0}, use_global_device_ids=true | all-gather | bytes 983040 | tf_op jit(solution)/shard_map/all_gather | solution.py:269
  61.8 2.9 %home_attention.1 = bf16[8,32,128]{2,1,0:T(8,128)(2,1)} custom-call(s32[1]{0:T(128)S(6)} %copy.16.place_ref, s32[4,8]{1,0:T(4,128)} %bitcast.16, s32[8]{0:T(128)} %length_ref.1, s32[4,8]{1,0:T(4,128)} %parent_ref.1, bf16[32,128]{1,0:T(8,128)(2,1)} %bitcast.14, bf16[1024,128]{1,0:T(8,128)(2,1)} %bitcast.12, bf16[64,128]{1,0:T(8,128)(2,1)} %bitcast.15, ...), custom_call_target="tpu_custom_call" | custom-call | tf_op jit(solution)/shard_map/home_attention/pallas_call | solution.py:289
  64.7 6.8 %all-to-all-start.2 = ((bf16[8,32,128]{2,1,0:T(8,128)(2,1)}), bf16[8,32,128]{2,1,0:T(8,128)(2,1)S(1)}, u32[]{:S(2)}, u32[]{:S(2)}) async-start(bf16[8,32,128]{2,1,0:T(8,128)(2,1)} %home_attention.1), calls=%async_computation.2 | async-start | bytes 131072 | tf_op jit(solution)/shard_map/all_to_all | solution.py:311
  71.5 0.0 copy-done.3
  71.6 7.2 %all-to-all-done.2.attended_ref = bf16[8,32,128]{2,1,0:T(8,128)(2,1)S(1)} async-done(((bf16[8,32,128]{2,1,0:T(8,128)(2,1)}), bf16[8,32,128]{2,1,0:T(8,128)(2,1)S(1)}, u32[]{:S(2)}, u32[]{:S(2)}) %all-to-all-start.2) | async-done | bytes 65568 | tf_op jit(solution)/shard_map/all_to_all | solution.py:311
  78.8 0.0 all-gather.2.cloned.1.call-done.weight_ref
  78.8 0.0 copy-done.2
  78.8 0.0 copy-done.1
  78.8 0.0 copy-start
  78.8 2.2 %copy-done = bf16[1024,2048]{1,0:T(8,128)(2,1)S(1)} copy-done((bf16[1024,2048]{1,0:T(8,128)(2,1)S(1)}, bf16[1024,2048]{1,0:T(8,128)(2,1)}, u32[]{:S(2)}) %copy-start) | copy-done | bytes 4194328
  81.0 1.9 %mix.1 = (bf16[4,3,8,128]{3,2,1,0:T(8,128)(2,1)}, bf16[32,2048]{1,0:T(8,128)(2,1)}) custom-call(bf16[8,32,128]{2,1,0:T(8,128)(2,1)S(1)} %all-to-all-done.2.attended_ref, bf16[1024,2048]{1,0:T(8,128)(2,1)S(1)} %copy-done, bf16[32,2048]{1,0:T(8,128)(2,1)S(1)} %bitcast.10, bf16[1,2048]{1,0:T(2,128)(2,1)S(1)} %reshape.31.gain_ref, bf16[3,2048,128]{2,1,0:T(8,128)(2,1)S(1)} %bitcast.9), custom_call_target="tpu_custom_call" | custom-call | tf_op jit(solution)/shard_map/mix/pallas_call | solution.py:312
  (1 shorter events, 0.0 us)
Async XLA Ops:
  7.2 64.4 %copy-start.3 = (bf16[2048]{0:T(1024)(128)(2,1)S(1)}, bf16[2048]{0:T(1024)(128)(2,1)}, u32[]{:S(2)}) copy-start(bf16[2048]{0:T(1024)(128)(2,1)} %param.26) | copy-start | bytes 12292
  7.2 71.6 %copy-start.2 = (bf16[4,8,2048]{2,1,0:T(8,128)(2,1)S(1)}, bf16[4,8,2048]{2,1,0:T(8,128)(2,1)}, u32[]{:S(2)}) copy-start(bf16[4,8,2048]{2,1,0:T(8,128)(2,1)} %param.16) | copy-start | bytes 393220
  7.2 71.6 %copy-start.1 = (bf16[2048,3,128]{2,0,1:T(8,128)(2,1)S(1)}, bf16[2048,3,128]{2,0,1:T(8,128)(2,1)}, u32[]{:S(2)}) copy-start(bf16[2048,3,128]{2,0,1:T(8,128)(2,1)} %param.27) | copy-start | bytes 4718596
  7.2 71.6 %all-gather.2.cloned.1.call-start = ((), (), s32[]{:S(2)}) async-start(), calls=%async_computation.3 | async-start | bytes 4718592 | tf_op jit(solution)/shard_map/all_gather | solution.py:271
  9.4 23.4 %all-to-all-start = ((bf16[32,32,128]{2,1,0:T(8,128)(2,1)}), bf16[32,32,128]{2,1,0:T(8,128)(2,1)S(1)}, u32[]{:S(2)}, u32[]{:S(2)}) async-start(bf16[32,32,128]{2,1,0:T(8,128)(2,1)} %broadcast_in_dim.2), calls=%async_computation | async-start | bytes 524288 | tf_op jit(solution)/shard_map/all_to_all | solution.py:268
  41.4 14.6 %all-to-all-start.1 = ((bf16[32,40,128]{2,1,0:T(8,128)(2,1)}), bf16[32,40,128]{2,1,0:T(8,128)(2,1)S(1)}, u32[]{:S(2)}, u32[]{:S(2)}) async-start(bf16[32,40,128]{2,1,0:T(8,128)(2,1)} %prompt_attention.1), calls=%async_computation.1 | async-start | bytes 655360 | tf_op jit(solution)/shard_map/all_to_all | solution.py:268
  64.7 14.1 %all-to-all-start.2 = ((bf16[8,32,128]{2,1,0:T(8,128)(2,1)}), bf16[8,32,128]{2,1,0:T(8,128)(2,1)S(1)}, u32[]{:S(2)}, u32[]{:S(2)}) async-start(bf16[8,32,128]{2,1,0:T(8,128)(2,1)} %home_attention.1), calls=%async_computation.2 | async-start | bytes 131072 | tf_op jit(solution)/shard_map/all_to_all | solution.py:311
  78.8 2.2 %copy-start = (bf16[1024,2048]{1,0:T(8,128)(2,1)S(1)}, bf16[1024,2048]{1,0:T(8,128)(2,1)}, u32[]{:S(2)}) copy-start(bf16[1024,2048]{1,0:T(8,128)(2,1)} %all-gather.2.cloned.1.call-done.weight_ref) | copy-start | bytes 12582916
Sparse Core Ops, SparseCore 0:
  10.1 62.6 all-gather.1

commit v2 on v1

--- a/solution.py
+++ b/solution.py
@@ -15,6 +15,7 @@
 SCORE_SCALE = 1.0 / math.sqrt(HEAD_DIM)
 LANES = 2 * HEAD_DIM
 STAT_ROWS = 8
+NOTE_ROWS = 16
 
 
 def split_heads(rows):
@@ -41,19 +42,33 @@
     return pltpu.roll(weights, 1, axis=1).astype(jnp.bfloat16)
 
 
-def prompt_kernel(owned_ref, live_ref, held_ref, cache_ref, out_ref, query_ref, sem):
-    owner = owned_ref[0]
-    chips = held_ref.shape[0] // 2
-    slot = (owner % 2) * chips + owner // 2
-    copy = pltpu.make_async_copy(held_ref.at[slot], query_ref, sem)
-    copy.start()
-    copy.wait()
-    rows = query_ref.shape[0]
-    queries = split_heads(query_ref[...])
-    cache = cache_ref[...]
+def prompt_kernel(asked_ref, slots_ref, out_ref):
+    core = lax.axis_index("req") % 2
+    rows = asked_ref.shape[1]
+    tokens = slots_ref.shape[1] - NOTE_ROWS
+    lane = lax.broadcasted_iota(jnp.int32, (NOTE_ROWS, LANES), 1)
+    row = lax.broadcasted_iota(jnp.int32, (NOTE_ROWS, LANES), 0)
+    for slot in range(2):
+        note = slots_ref[slot, tokens:].astype(jnp.float32)
+
+        def number(index):
+            here = jnp.logical_and(row == 0, lane == index)
+            return jnp.sum(jnp.where(here, note, 0.0)).astype(jnp.int32)
+
+        owner = number(0)
+        live = number(1) * 16 + number(2)
+
+        @pl.when(owner % 2 == core)
+        def _():
+            chip = owner // 2
+            out_ref[chip] = prompt_packet(asked_ref[chip], slots_ref[slot, :tokens], live, rows)
+
+
+def prompt_packet(query_rows, cache, live, rows):
+    queries = split_heads(query_rows)
     scores = dot_rows(queries, cache) * SCORE_SCALE
     column = lax.broadcasted_iota(jnp.int32, scores.shape, 1)
-    valid = jnp.logical_and(column % 2 == 0, column < 2 * live_ref[0])
+    valid = jnp.logical_and(column % 2 == 0, column < 2 * live)
     scores = jnp.where(valid, scores, NEG_FILL)
     top = jnp.max(scores, axis=1, keepdims=True)
     weights = jnp.exp(scores - top).astype(jnp.bfloat16).astype(jnp.float32)
@@ -75,31 +90,40 @@
     second = jnp.sum(jnp.where(on_row, low, 0.0), axis=0, keepdims=True)
     stat_row = lax.broadcasted_iota(jnp.int32, (STAT_ROWS, LANES), 0)
     stats = jnp.where(stat_row == 0, first, jnp.where(stat_row == 1, second, 0.0))
-    packet = jnp.concatenate([mean.astype(jnp.float32), stats], axis=0).astype(jnp.bfloat16)
-    for index in range(out_ref.shape[0]):
-        out_ref[index] = packet
+    return jnp.concatenate([mean.astype(jnp.float32), stats], axis=0).astype(jnp.bfloat16)
 
 
 def home_kernel(
-    place_ref,
+    owned_ref,
+    live_ref,
     table_ref,
     length_ref,
     parent_ref,
     query_ref,
     home_ref,
     fresh_ref,
-    result_ref,
-    out_ref,
+    prompt_ref,
+    mean_ref,
+    level_ref,
+    slot_ref,
     root_ref,
     line_ref,
-    packet_ref,
-    sem,
+    note_ref,
+    sems,
 ):
-    place = place_ref[0]
-    chips = result_ref.shape[0] // 2
-    slot = (place % 2) * chips + place // 2
-    copy = pltpu.make_async_copy(result_ref.at[slot], packet_ref, sem)
-    copy.start()
+    tokens = prompt_ref.shape[0]
+    note_lane = lax.broadcasted_iota(jnp.int32, (NOTE_ROWS, LANES), 1)
+    live = live_ref[0]
+    note = jnp.where(
+        note_lane == 0, owned_ref[0], jnp.where(note_lane == 1, live // 16, live % 16)
+    )
+    note_ref[...] = note.astype(jnp.float32).astype(jnp.bfloat16)
+    copies = [
+        pltpu.make_async_copy(prompt_ref, slot_ref.at[pl.ds(0, tokens)], sems.at[0]),
+        pltpu.make_async_copy(note_ref, slot_ref.at[pl.ds(tokens, NOTE_ROWS)], sems.at[1]),
+    ]
+    for copy in copies:
+        copy.start()
     step_count = parent_ref.shape[0]
     block_count = table_ref.shape[0]
     rows = query_ref.shape[0]
@@ -181,48 +205,56 @@
         to_value_rows(fresh_weights), fresh, preferred_element_type=jnp.float32
     )
 
-    copy.wait()
-    packet = packet_ref[...].astype(jnp.float32)
-    mean = packet[:rows]
+    mean_ref[...] = join_heads(numer / total)
+    level = jnp.broadcast_to(top + jnp.log(total), numer.shape)
+    level_ref[...] = join_heads(level)
+    for copy in copies:
+        copy.wait()
+
+
+def combine_kernel(place_ref, mean_ref, level_ref, result_ref, weight_ref, out_ref):
+    rows = mean_ref.shape[0]
+    packet = result_ref[place_ref[0] // 2].astype(jnp.float32)
     wide = (2 * rows, LANES)
-    wide_lane = lax.broadcasted_iota(jnp.int32, wide, 1)
-    wide_row = lax.broadcasted_iota(jnp.int32, wide, 0)
-    on_row = wide_lane % HEAD_DIM == wide_row
-    low_half = wide_lane < HEAD_DIM
-    level = jnp.sum(
-        jnp.where(on_row, jnp.broadcast_to(packet[rows : rows + 1], wide), 0.0),
-        axis=1,
-        keepdims=True,
-    ) + jnp.sum(
-        jnp.where(
-            jnp.logical_and(on_row, low_half),
-            jnp.broadcast_to(packet[rows + 1 : rows + 2], wide),
-            0.0,
-        ),
-        axis=1,
-        keepdims=True,
-    )
-    joint_top = jnp.maximum(top, level)
-    home_factor = jnp.exp(top - joint_top)
-    prompt_factor = jnp.exp(level - joint_top)
-    both = jnp.concatenate([mean, mean], axis=0)
-    attended = (numer * home_factor + both * prompt_factor) / (
-        total * home_factor + prompt_factor
-    )
-    attended = join_heads(attended).astype(jnp.bfloat16)
+    lane = lax.broadcasted_iota(jnp.int32, wide, 1)
+    row = lax.broadcasted_iota(jnp.int32, wide, 0)
+    on_row = lane % HEAD_DIM == row
+    terms = jnp.broadcast_to(packet[rows : rows + 1], wide) + jnp.where(
+        lane < HEAD_DIM, jnp.broadcast_to(packet[rows + 1 : rows + 2], wide), 0.0
+    )
+    prompt_level = jnp.sum(jnp.where(on_row, terms, 0.0), axis=1, keepdims=True)
+    prompt_level = join_heads(jnp.broadcast_to(prompt_level, wide))
+    level = level_ref[...]
+    joint_top = jnp.maximum(level, prompt_level)
+    home_factor = jnp.exp(level - joint_top)
+    prompt_factor = jnp.exp(prompt_level - joint_top)
+    attended = (mean_ref[...] * home_factor + packet[:rows] * prompt_factor) / (
+        home_factor + prompt_factor
+    )
+    partial = jnp.dot(
+        attended.astype(jnp.bfloat16), weight_ref[...], preferred_element_type=jnp.float32
+    )
+    width = out_ref.shape[2]
     for index in range(out_ref.shape[0]):
-        out_ref[index] = attended
-
-
-def mix_kernel(
-    attended_ref, weight_ref, residual_ref, gain_ref, qkv_weight_ref, qkv_ref, residual_out_ref
-):
-    shard_count = attended_ref.shape[0]
-    attended = jnp.concatenate([attended_ref[index] for index in range(shard_count)], axis=1)
-    mixed = residual_ref[...].astype(jnp.float32) + jnp.dot(
-        attended, weight_ref[...], preferred_element_type=jnp.float32
-    )
-    residual_out_ref[...] = mixed.astype(jnp.bfloat16)
+        out_ref[index] = partial[:, index * width : (index + 1) * width].astype(out_ref.dtype)
+
+
+def sum_kernel(partial_ref, residual_ref, out_ref):
+    width = partial_ref.shape[2]
+    first = pl.multiple_of(lax.axis_index("tp") * width, width)
+    mixed = residual_ref[:, pl.ds(first, width)].astype(jnp.float32)
+    for index in range(partial_ref.shape[0]):
+        mixed = mixed + partial_ref[index].astype(jnp.float32)
+    mixed = mixed.astype(jnp.bfloat16)
+    for index in range(out_ref.shape[0]):
+        out_ref[index] = mixed
+
+
+def project_kernel(mixed_ref, gain_ref, qkv_weight_ref, qkv_ref, residual_out_ref):
+    shard_count = mixed_ref.shape[0]
+    rounded = jnp.concatenate([mixed_ref[index] for index in range(shard_count)], axis=1)
+    residual_out_ref[...] = rounded
+    mixed = rounded.astype(jnp.float32)
     mean_square = jnp.mean(mixed * mixed, axis=1, keepdims=True)
     gain = gain_ref[...].astype(jnp.float32)
     normed = (mixed * lax.rsqrt(mean_square + NORM_EPS) * gain).astype(jnp.bfloat16)
@@ -236,6 +268,7 @@
 
 VMEM_SPEC = pl.BlockSpec(memory_space=pltpu.VMEM)
 SMEM_SPEC = pl.BlockSpec(memory_space=pltpu.SMEM)
+KERNEL_PARAMS = pltpu.CompilerParams(vmem_limit_bytes=20 * 1024 * 1024)
 ANY_SPEC = pl.BlockSpec(memory_space=pl.ANY)
 
 
@@ -265,64 +298,87 @@
     same_chip = [[2 * chip, 2 * chip + 1] for chip in range(chips)]
 
     def route(slots):
-        arrived = lax.all_to_all(slots, "req", 0, 0, axis_index_groups=same_core)
-        return lax.all_gather(arrived, "req", axis_index_groups=same_chip, tiled=True)
-
-    whole_weight = lax.all_gather(out_weight, "tp", axis=0, tiled=True)
+        return lax.all_to_all(slots, "req", 0, 0, axis_index_groups=same_core)
 
     query_rows = queries.reshape(rows, lane_count)
-    held = route(jnp.broadcast_to(query_rows[None], (chips, rows, lane_count)))
-    prompt_rows = prompt_cache.reshape(-1, lane_count)
-    packet_rows = rows + STAT_ROWS
-    results = pl.pallas_call(
-        prompt_kernel,
-        out_shape=jax.ShapeDtypeStruct((chips, packet_rows, lane_count), jnp.bfloat16),
-        in_specs=[SMEM_SPEC, SMEM_SPEC, ANY_SPEC, VMEM_SPEC],
-        out_specs=VMEM_SPEC,
-        scratch_shapes=[pltpu.VMEM((rows, lane_count), jnp.bfloat16), pltpu.SemaphoreType.DMA],
-        name="prompt_attention",
-    )(owned_request, prompt_len, held, prompt_rows)
-    returned = route(results)
+    asked = route(jnp.broadcast_to(query_rows[None], (chips, rows, lane_count)))
 
     home_rows = home_cache.reshape(-1, lane_count)
     fresh_rows = new_kv.reshape(-1, lane_count)
-    attended = pl.pallas_call(
+    prompt_rows = prompt_cache.reshape(-1, lane_count)
+    slot_rows = prompt_rows.shape[0] + NOTE_ROWS
+    home_mean, home_level, own_slot = pl.pallas_call(
         home_kernel,
-        out_shape=jax.ShapeDtypeStruct((tp_size, rows, lane_count), jnp.bfloat16),
-        in_specs=[SMEM_SPEC] * 4 + [VMEM_SPEC] * 3 + [ANY_SPEC],
-        out_specs=VMEM_SPEC,
+        out_shape=(
+            jax.ShapeDtypeStruct((rows, lane_count), jnp.float32),
+            jax.ShapeDtypeStruct((rows, lane_count), jnp.float32),
+            jax.ShapeDtypeStruct((slot_rows, lane_count), jnp.bfloat16),
+        ),
+        in_specs=[SMEM_SPEC] * 5 + [VMEM_SPEC] * 3 + [ANY_SPEC],
+        out_specs=(VMEM_SPEC, VMEM_SPEC, ANY_SPEC),
         scratch_shapes=[
             pltpu.SMEM((step_count, BEAMS), jnp.int32),
             pltpu.SMEM((step_count * step_count, BEAMS), jnp.int32),
-            pltpu.VMEM((packet_rows, lane_count), jnp.bfloat16),
-            pltpu.SemaphoreType.DMA,
+            pltpu.VMEM((NOTE_ROWS, lane_count), jnp.bfloat16),
+            pltpu.SemaphoreType.DMA((2,)),
         ],
+        compiler_params=KERNEL_PARAMS,
         name="home_attention",
     )(
-        prompt_place,
+        owned_request,
+        prompt_len,
         home_table.T,
         home_len,
         parents,
         query_rows,
         home_rows,
         fresh_rows,
-        returned,
-    )
-    all_heads = lax.all_to_all(attended, "tp", 0, 0)
+        prompt_rows,
+    )
+    both_slots = lax.all_gather(own_slot, "req", axis_index_groups=same_chip)
+
+    packet_rows = rows + STAT_ROWS
+    results = pl.pallas_call(
+        prompt_kernel,
+        out_shape=jax.ShapeDtypeStruct((chips, packet_rows, lane_count), jnp.bfloat16),
+        in_specs=[VMEM_SPEC] * 2,
+        out_specs=VMEM_SPEC,
+        compiler_params=KERNEL_PARAMS,
+        name="prompt_attention",
+    )(asked, both_slots)
+    returned = route(results)
+
+    width = model_width // tp_size
+    partial = pl.pallas_call(
+        combine_kernel,
+        out_shape=jax.ShapeDtypeStruct((tp_size, rows, width), jnp.float32),
+        in_specs=[SMEM_SPEC] + [VMEM_SPEC] * 4,
+        out_specs=VMEM_SPEC,
+        compiler_params=KERNEL_PARAMS,
+        name="combine",
+    )(prompt_place, home_mean, home_level, returned, out_weight)
+    partials = lax.all_to_all(partial, "tp", 0, 0)
+    mixed = pl.pallas_call(
+        sum_kernel,
+        out_shape=jax.ShapeDtypeStruct((tp_size, rows, width), jnp.bfloat16),
+        in_specs=[VMEM_SPEC, VMEM_SPEC],
+        out_specs=VMEM_SPEC,
+        compiler_params=KERNEL_PARAMS,
+        name="add_shards",
+    )(partials, residual.reshape(rows, model_width))
+    all_mixed = lax.all_to_all(mixed, "tp", 0, 0)
     next_qkv, new_residual = pl.pallas_call(
-        mix_kernel,
+        project_kernel,
         out_shape=(
             jax.ShapeDtypeStruct((step_count, 3, row_count, lane_count), jnp.bfloat16),
             jax.ShapeDtypeStruct((rows, model_width), jnp.bfloat16),
         ),
-        in_specs=[VMEM_SPEC] * 5,
+        in_specs=[VMEM_SPEC] * 3,
         out_specs=(VMEM_SPEC, VMEM_SPEC),
-        compiler_params=pltpu.CompilerParams(vmem_limit_bytes=40 * 1024 * 1024),
-        name="mix",
+        compiler_params=KERNEL_PARAMS,
+        name="project",
     )(
-        all_heads,
-        whole_weight,
-        residual.reshape(rows, model_width),
+        all_mixed,
         norm_gain.reshape(1, model_width),
         qkv_weight.transpose(1, 0, 2),
     )

time: 90.3 us -> 84.4 us (0.935)
  the two profiles are of different devices: /device:TPU:1 before, /device:TPU:64 now
where the time goes in v2:
time: 84.4 us; the launch traced here: 83.7 us
  waiting for transfers between devices  24.9 us (30%)
  starting transfers between devices  23.5 us (28%)
  blocking collectives  20.7 us (25%)
  local copies, waits for them, and re-layouts  6.85 us (8%)
  Pallas kernels  4.96 us (6%)
  between operations  2.65 us (3%)
    all_to_all x2, starting transfers between devices, route(): return lax.all_to_all(slots, 'req', 0, 0, axis_index_groups=same_core)  20.2 us
    all_to_all x1, blocking collectives, shards(): partials = lax.all_to_all(partial, 'tp', 0, 0)  18.5 us
    all_to_all x2, waiting for transfers between devices, route(): return lax.all_to_all(slots, 'req', 0, 0, axis_index_groups=same_core)  16 us
    all_to_all x1, waiting for transfers between devices, shards(): all_mixed = lax.all_to_all(mixed, 'tp', 0, 0)  8.97 us
    unnamed x22, local copies, waits for them, and re-layouts  5.4 us
    all_to_all x1, starting transfers between devices, shards(): all_mixed = lax.all_to_all(mixed, 'tp', 0, 0)  3.37 us
    all_gather x1, blocking collectives, shards(): both_slots = lax.all_gather(own_slot, 'req', axis_index_groups=same_chip)  2.19 us
  transfers between devices with their start and end apart: 3, of which 3 were waited for; matrix products, arithmetic and copies ran while one was open for 0% of the time, Pallas kernels for 2%

profile of v2, /device:TPU:64, one launch (start us, length us, event | category | flops | bytes accessed | tf_op | source)
XLA Modules:
  0.0 83.7 jit_solution(12438439973799807054)
XLA Ops:
  0.6 1.4 %broadcast_in_dim.2 = bf16[32,32,128]{2,1,0:T(8,128)(2,1)} broadcast(bf16[32,128]{1,0:T(8,128)(2,1)} %bitcast.15), dimensions={1,2} | broadcast | bytes 270336 | tf_op jit(solution)/shard_map/broadcast_in_dim | solution.py:304
  2.1 12.6 %all-to-all-start = ((bf16[32,32,128]{2,1,0:T(8,128)(2,1)}), bf16[32,32,128]{2,1,0:T(8,128)(2,1)S(1)}, u32[]{:S(2)}, u32[]{:S(2)}) async-start(bf16[32,32,128]{2,1,0:T(8,128)(2,1)} %broadcast_in_dim.2), calls=%async_computation | async-start | bytes 524288 | tf_op jit(solution)/shard_map/all_to_all | solution.py:301
  16.0 0.0 copy-start.1
  16.0 0.0 copy-start.2
  16.0 1.0 %copy-done.2 = bf16[4,128,2,128]{3,2,1,0:T(2,128)(2,1)S(1)} copy-done((bf16[4,128,2,128]{3,2,1,0:T(2,128)(2,1)S(1)}, bf16[4,128,2,128]{3,2,1,0:T(2,128)(2,1)}, u32[]{:S(2)}) %copy-start.2) | copy-done | bytes 262168
  17.0 0.0 copy-start.3
  17.0 0.9 %copy-done.3 = bf16[4,128,2,128]{3,2,1,0:T(2,128)(2,1)S(1)} copy-done((bf16[4,128,2,128]{3,2,1,0:T(2,128)(2,1)S(1)}, bf16[4,128,2,128]{3,2,1,0:T(2,128)(2,1)}, u32[]{:S(2)}) %copy-start.3) | copy-done | bytes 262168
  17.9 0.0 copy-start.5
  17.9 0.7 copy-done.5
  18.6 0.0 copy-start.6
  18.6 0.7 copy-done.6
  19.3 0.0 copy-start.7
  19.3 0.7 copy-done.7
  20.0 0.0 copy-start.8
  20.0 0.7 copy-done.8
  20.7 0.0 copy-start.9
  20.7 0.7 copy-done.9
  21.4 1.4 %home_attention.1 = (f32[32,128]{1,0:T(8,128)S(1)}, f32[32,128]{1,0:T(8,128)S(1)}, bf16[1040,128]{1,0:T(8,128)(2,1)S(1)}) custom-call(s32[1]{0:T(128)S(6)} %copy.17.owned_ref, s32[1]{0:T(128)S(6)} %copy.18.live_ref, s32[4,8]{1,0:T(4,128)S(1)} %bitcast.18, s32[8]{0:T(128)S(1)} %copy-done.9, s32[4,8]{1,0:T(4,128)S(1)} %copy-done.8, ...), custom_call_target="tpu_custom_call" | custom-call | tf_op jit(solution)/shard_map/home_attention/pallas_call | solution.py:310
  22.8 2.2 %all-gather = bf16[2080,128]{1,0:T(8,128)(2,1)S(1)} all-gather(bf16[1040,128]{1,0:T(8,128)(2,1)S(1)} %get-tuple-element.9), channel_id=2, replica_groups={{0,8},{16,24},{32,40},{48,56},{64,72},{80,88},{96,104},{112,120},{128,1..., dimensions={0}, use_global_device_ids=true | all-gather | bytes 798720 | tf_op jit(solution)/shard_map/all_gather | solution.py:338
  25.0 2.0 %all-to-all-done.asked_ref = bf16[32,32,128]{2,1,0:T(8,128)(2,1)S(1)} async-done(((bf16[32,32,128]{2,1,0:T(8,128)(2,1)}), bf16[32,32,128]{2,1,0:T(8,128)(2,1)S(1)}, u32[]{:S(2)}, u32[]{:S(2)}) %all-to-all-start) | async-done | bytes 262176 | tf_op jit(solution)/shard_map/all_to_all | solution.py:301
  26.9 0.0 copy-start.4
  26.9 1.5 %prompt_attention.1 = bf16[32,40,128]{2,1,0:T(8,128)(2,1)} custom-call(bf16[32,32,128]{2,1,0:T(8,128)(2,1)S(1)} %all-to-all-done.asked_ref, bf16[2,1040,128]{2,1,0:T(8,128)(2,1)S(1)} %bitcast.10), custom_call_target="tpu_custom_call" | custom-call | tf_op jit(solution)/shard_map/prompt_attention/pallas_call | solution.py:341
  28.5 0.0 copy-start.10
  28.5 0.0 copy-start
  28.5 7.6 %all-to-all-start.1 = ((bf16[32,40,128]{2,1,0:T(8,128)(2,1)}), bf16[32,40,128]{2,1,0:T(8,128)(2,1)S(1)}, u32[]{:S(2)}, u32[]{:S(2)}) async-start(bf16[32,40,128]{2,1,0:T(8,128)(2,1)} %prompt_attention.1), calls=%async_computation.1 | async-start | bytes 655360 | tf_op jit(solution)/shard_map/all_to_all | solution.py:301
  36.7 14.0 %all-to-all-done.1.result_ref = bf16[32,40,128]{2,1,0:T(8,128)(2,1)S(1)} async-done(((bf16[32,40,128]{2,1,0:T(8,128)(2,1)}), bf16[32,40,128]{2,1,0:T(8,128)(2,1)S(1)}, u32[]{:S(2)}, u32[]{:S(2)}) %all-to-all-start.1) | async-done | bytes 327712 | tf_op jit(solution)/shard_map/all_to_all | solution.py:301
  50.7 0.0 copy-done.1
  50.7 0.3 combine.1
  51.0 18.5 %all_to_all.20.partial_ref = f32[8,32,256]{2,1,0:T(8,128)S(1)} all-to-all(f32[8,32,256]{2,1,0:T(8,128)S(1)} %combine.1), channel_id=1, replica_groups=mesh['req'=64,'tp'=8] {'tp'}, dimensions={0} | all-to-all | bytes 524288 | tf_op jit(solution)/shard_map/all_to_all | solution.py:360
  69.5 0.0 copy-done.4
  69.5 0.7 add_shards.1
  70.2 3.4 %all-to-all-start.3 = ((bf16[8,32,256]{2,1,0:T(8,128)(2,1)}), bf16[8,32,256]{2,1,0:T(8,128)(2,1)S(1)}, u32[]{:S(2)}, u32[]{:S(2)}) async-start(bf16[8,32,256]{2,1,0:T(8,128)(2,1)} %add_shards.1), calls=%async_computation.3 | async-start | bytes 262144 | tf_op jit(solution)/shard_map/all_to_all | solution.py:369
  73.6 0.0 copy-done.10
  73.6 9.0 %all-to-all-done.3.mixed_ref = bf16[8,32,256]{2,1,0:T(8,128)(2,1)S(1)} async-done(((bf16[8,32,256]{2,1,0:T(8,128)(2,1)}), bf16[8,32,256]{2,1,0:T(8,128)(2,1)S(1)}, u32[]{:S(2)}, u32[]{:S(2)}) %all-to-all-start.3) | async-done | bytes 131104 | tf_op jit(solution)/shard_map/all_to_all | solution.py:369
  82.6 0.0 copy-done
  82.6 1.1 %project.1 = (bf16[4,3,8,128]{3,2,1,0:T(8,128)(2,1)}, bf16[32,2048]{1,0:T(8,128)(2,1)}) custom-call(bf16[8,32,256]{2,1,0:T(8,128)(2,1)S(1)} %all-to-all-done.3.mixed_ref, bf16[1,2048]{1,0:T(2,128)(2,1)S(1)} %reshape.31.gain_ref, bf16[3,2048,128]{2,1,0:T(8,128)(2,1)S(1)} %bitcast.11), custom_call_target="tpu_custom_call" | custom-call | tf_op jit(solution)/shard_map/project/pallas_call | solution.py:370
  (1 shorter events, 0.0 us)
Async XLA Ops:
  2.1 24.9 %all-to-all-start = ((bf16[32,32,128]{2,1,0:T(8,128)(2,1)}), bf16[32,32,128]{2,1,0:T(8,128)(2,1)S(1)}, u32[]{:S(2)}, u32[]{:S(2)}) async-start(bf16[32,32,128]{2,1,0:T(8,128)(2,1)} %broadcast_in_dim.2), calls=%async_computation | async-start | bytes 524288 | tf_op jit(solution)/shard_map/all_to_all | solution.py:301
  16.0 34.8 %copy-start.1 = (bf16[128,2048]{1,0:T(8,128)(2,1)S(1)}, bf16[128,2048]{1,0:T(8,128)(2,1)}, u32[]{:S(2)}) copy-start(bf16[128,2048]{1,0:T(8,128)(2,1)} %weight_ref.1) | copy-start | bytes 1572868
  16.0 1.0 %copy-start.2 = (bf16[4,128,2,128]{3,2,1,0:T(2,128)(2,1)S(1)}, bf16[4,128,2,128]{3,2,1,0:T(2,128)(2,1)}, u32[]{:S(2)}) copy-start(bf16[4,128,2,128]{3,2,1,0:T(2,128)(2,1)} %param.17) | copy-start | bytes 786436
  17.0 0.9 %copy-start.3 = (bf16[4,128,2,128]{3,2,1,0:T(2,128)(2,1)S(1)}, bf16[4,128,2,128]{3,2,1,0:T(2,128)(2,1)}, u32[]{:S(2)}) copy-start(bf16[4,128,2,128]{3,2,1,0:T(2,128)(2,1)} %param.18) | copy-start | bytes 786436
  17.9 0.7 copy-start.5
  18.6 0.7 copy-start.6
  19.3 0.7 copy-start.7
  20.0 0.7 copy-start.8
  20.7 0.7 copy-start.9
  26.9 42.6 %copy-start.4 = (bf16[4,8,2048]{2,1,0:T(8,128)(2,1)S(1)}, bf16[4,8,2048]{2,1,0:T(8,128)(2,1)}, u32[]{:S(2)}) copy-start(bf16[4,8,2048]{2,1,0:T(8,128)(2,1)} %param.16) | copy-start | bytes 393220
  28.5 45.1 %copy-start.10 = (bf16[2048]{0:T(1024)(128)(2,1)S(1)}, bf16[2048]{0:T(1024)(128)(2,1)}, u32[]{:S(2)}) copy-start(bf16[2048]{0:T(1024)(128)(2,1)} %param.26) | copy-start | bytes 12292
  28.5 54.1 %copy-start = (bf16[2048,3,128]{2,0,1:T(8,128)(2,1)S(1)}, bf16[2048,3,128]{2,0,1:T(8,128)(2,1)}, u32[]{:S(2)}) copy-start(bf16[2048,3,128]{2,0,1:T(8,128)(2,1)} %param.27) | copy-start | bytes 4718596
  28.5 22.2 %all-to-all-start.1 = ((bf16[32,40,128]{2,1,0:T(8,128)(2,1)}), bf16[32,40,128]{2,1,0:T(8,128)(2,1)S(1)}, u32[]{:S(2)}, u32[]{:S(2)}) async-start(bf16[32,40,128]{2,1,0:T(8,128)(2,1)} %prompt_attention.1), calls=%async_computation.1 | async-start | bytes 655360 | tf_op jit(solution)/shard_map/all_to_all | solution.py:301
  70.2 12.4 %all-to-all-start.3 = ((bf16[8,32,256]{2,1,0:T(8,128)(2,1)}), bf16[8,32,256]{2,1,0:T(8,128)(2,1)S(1)}, u32[]{:S(2)}, u32[]{:S(2)}) async-start(bf16[8,32,256]{2,1,0:T(8,128)(2,1)} %add_shards.1), calls=%async_computation.3 | async-start | bytes 262144 | tf_op jit(solution)/shard_map/all_to_all | solution.py:369

commit v3 on v2

--- a/solution.py
+++ b/solution.py
@@ -40,6 +40,17 @@
 
 def to_value_rows(weights):
     return pltpu.roll(weights, 1, axis=1).astype(jnp.bfloat16)
+
+
+def fill_kernel(query_ref, out_ref, sems):
+    copies = [
+        pltpu.make_async_copy(query_ref, out_ref.at[index], sems.at[index])
+        for index in range(out_ref.shape[0])
+    ]
+    for copy in copies:
+        copy.start()
+    for copy in copies:
+        copy.wait()
 
 
 def prompt_kernel(asked_ref, slots_ref, out_ref):
@@ -96,6 +107,7 @@
 def home_kernel(
     owned_ref,
     live_ref,
+    place_ref,
     table_ref,
     length_ref,
     parent_ref,
@@ -103,8 +115,10 @@
     home_ref,
     fresh_ref,
     prompt_ref,
+    gain_ref,
     mean_ref,
     level_ref,
+    gain_row_ref,
     slot_ref,
     root_ref,
     line_ref,
@@ -207,14 +221,17 @@
 
     mean_ref[...] = join_heads(numer / total)
     level = jnp.broadcast_to(top + jnp.log(total), numer.shape)
-    level_ref[...] = join_heads(level)
+    level_ref[:rows] = join_heads(level)
+    level_ref[rows:] = jnp.full((BEAMS, LANES), place_ref[0]).astype(jnp.float32)
+    gain_row_ref[...] = gain_ref[...].astype(jnp.float32)
     for copy in copies:
         copy.wait()
 
 
-def combine_kernel(place_ref, mean_ref, level_ref, result_ref, weight_ref, out_ref):
+def combine_kernel(mean_ref, level_ref, result_ref, weight_ref, out_ref):
     rows = mean_ref.shape[0]
-    packet = result_ref[place_ref[0] // 2].astype(jnp.float32)
+    place = jnp.max(level_ref[rows:]).astype(jnp.int32)
+    packet = result_ref[place // 2].astype(jnp.float32)
     wide = (2 * rows, LANES)
     lane = lax.broadcasted_iota(jnp.int32, wide, 1)
     row = lax.broadcasted_iota(jnp.int32, wide, 0)
@@ -224,7 +241,7 @@
     )
     prompt_level = jnp.sum(jnp.where(on_row, terms, 0.0), axis=1, keepdims=True)
     prompt_level = join_heads(jnp.broadcast_to(prompt_level, wide))
-    level = level_ref[...]
+    level = level_ref[:rows]
     joint_top = jnp.maximum(level, prompt_level)
     home_factor = jnp.exp(level - joint_top)
     prompt_factor = jnp.exp(prompt_level - joint_top)
@@ -256,8 +273,7 @@
     residual_out_ref[...] = rounded
     mixed = rounded.astype(jnp.float32)
     mean_square = jnp.mean(mixed * mixed, axis=1, keepdims=True)
-    gain = gain_ref[...].astype(jnp.float32)
-    normed = (mixed * lax.rsqrt(mean_square + NORM_EPS) * gain).astype(jnp.bfloat16)
+    normed = (mixed * lax.rsqrt(mean_square + NORM_EPS) * gain_ref[...]).astype(jnp.bfloat16)
     for kind in range(qkv_weight_ref.shape[0]):
         projected = jnp.dot(
             normed, qkv_weight_ref[kind], preferred_element_type=jnp.float32
@@ -301,32 +317,42 @@
         return lax.all_to_all(slots, "req", 0, 0, axis_index_groups=same_core)
 
     query_rows = queries.reshape(rows, lane_count)
-    asked = route(jnp.broadcast_to(query_rows[None], (chips, rows, lane_count)))
+    asked = route(
+        pl.pallas_call(
+            fill_kernel,
+            out_shape=jax.ShapeDtypeStruct((chips, rows, lane_count), jnp.bfloat16),
+            in_specs=[ANY_SPEC],
+            out_specs=ANY_SPEC,
+            scratch_shapes=[pltpu.SemaphoreType.DMA((chips,))],
+            name="fill_slots",
+        )(query_rows)
+    )
 
     home_rows = home_cache.reshape(-1, lane_count)
     fresh_rows = new_kv.reshape(-1, lane_count)
     prompt_rows = prompt_cache.reshape(-1, lane_count)
     slot_rows = prompt_rows.shape[0] + NOTE_ROWS
-    home_mean, home_level, own_slot = pl.pallas_call(
+    home_mean, home_level, gain_row, own_slot = pl.pallas_call(
         home_kernel,
         out_shape=(
             jax.ShapeDtypeStruct((rows, lane_count), jnp.float32),
-            jax.ShapeDtypeStruct((rows, lane_count), jnp.float32),
+            jax.ShapeDtypeStruct((rows + BEAMS, lane_count), jnp.float32),
+            jax.ShapeDtypeStruct((1, model_width), jnp.float32),
             jax.ShapeDtypeStruct((slot_rows, lane_count), jnp.bfloat16),
         ),
-        in_specs=[SMEM_SPEC] * 5 + [VMEM_SPEC] * 3 + [ANY_SPEC],
-        out_specs=(VMEM_SPEC, VMEM_SPEC, ANY_SPEC),
+        in_specs=[SMEM_SPEC] * 6 + [VMEM_SPEC] * 3 + [ANY_SPEC, VMEM_SPEC],
+        out_specs=(VMEM_SPEC, VMEM_SPEC, VMEM_SPEC, ANY_SPEC),
         scratch_shapes=[
             pltpu.SMEM((step_count, BEAMS), jnp.int32),
             pltpu.SMEM((step_count * step_count, BEAMS), jnp.int32),
             pltpu.VMEM((NOTE_ROWS, lane_count), jnp.bfloat16),
             pltpu.SemaphoreType.DMA((2,)),
         ],
-        compiler_params=KERNEL_PARAMS,
         name="home_attention",
     )(
         owned_request,
         prompt_len,
+        prompt_place,
         home_table.T,
         home_len,
         parents,
@@ -334,13 +360,14 @@
         home_rows,
         fresh_rows,
         prompt_rows,
+        norm_gain.reshape(1, model_width),
     )
     both_slots = lax.all_gather(own_slot, "req", axis_index_groups=same_chip)
 
     packet_rows = rows + STAT_ROWS
     results = pl.pallas_call(
         prompt_kernel,
-        out_shape=jax.ShapeDtypeStruct((chips, packet_rows, lane_count), jnp.bfloat16),
+        out_shape=pltpu.VMEM((chips, packet_rows, lane_count), jnp.bfloat16),
         in_specs=[VMEM_SPEC] * 2,
         out_specs=VMEM_SPEC,
         compiler_params=KERNEL_PARAMS,
@@ -352,11 +379,11 @@
     partial = pl.pallas_call(
         combine_kernel,
         out_shape=jax.ShapeDtypeStruct((tp_size, rows, width), jnp.float32),
-        in_specs=[SMEM_SPEC] + [VMEM_SPEC] * 4,
+        in_specs=[VMEM_SPEC] * 4,
         out_specs=VMEM_SPEC,
         compiler_params=KERNEL_PARAMS,
         name="combine",
-    )(prompt_place, home_mean, home_level, returned, out_weight)
+    )(home_mean, home_level, returned, out_weight)
     partials = lax.all_to_all(partial, "tp", 0, 0)
     mixed = pl.pallas_call(
         sum_kernel,
@@ -379,7 +406,7 @@
         name="project",
     )(
         all_mixed,
-        norm_gain.reshape(1, model_width),
+        gain_row,
         qkv_weight.transpose(1, 0, 2),
     )
     return (

time: 84.4 us -> 93.6 us (1.11)
  the two profiles are of different devices: /device:TPU:64 before, /device:TPU:6 now
where the time goes in v3:
time: 93.6 us; the launch traced here: 92 us
  blocking collectives  51.7 us (55%)
  Pallas kernels  22.8 us (24%)
  starting transfers between devices  13.5 us (14%)
  between operations  2.65 us (3%)
  local copies, waits for them, and re-layouts  1.32 us (1%)
    all_to_all x1, blocking collectives, route(): return lax.all_to_all(slots, 'req', 0, 0, axis_index_groups=same_core)  20.5 us
    all_to_all x1, blocking collectives, shards(): partials = lax.all_to_all(partial, 'tp', 0, 0)  17.4 us
    all_to_all x1, starting transfers between devices, route(): return lax.all_to_all(slots, 'req', 0, 0, axis_index_groups=same_core)  13.5 us
    all_to_all x1, blocking collectives, shards(): all_mixed = lax.all_to_all(mixed, 'tp', 0, 0)  11.5 us
    pallas_call x1, Pallas kernels, shards(): pl.pallas_call(home_kernel, out_shape=(jax.ShapeDtypeStruct((rows, lane_c...  10.7 us
    pallas_call x1, Pallas kernels, shards(): pl.pallas_call(fill_kernel, out_shape=jax.ShapeDtypeStruct((chips, rows,...  9.34 us
    all_gather x1, blocking collectives, shards(): both_slots = lax.all_gather(own_slot, 'req', axis_index_groups=same_chip)  2.4 us
  transfers between devices with their start and end apart: 1, of which 0 were waited for; matrix products, arithmetic and copies ran while one was open for 1% of the time, Pallas kernels for 12%

profile of v3, /device:TPU:6, one launch (start us, length us, event | category | flops | bytes accessed | tf_op | source)
XLA Modules:
  0.0 92.0 jit_solution(228304670149779381)
XLA Ops:
  0.6 9.3 %fill_slots.1 = bf16[32,32,128]{2,1,0:T(8,128)(2,1)} custom-call(bf16[32,128]{1,0:T(8,128)(2,1)} %bitcast.15), custom_call_target="tpu_custom_call" | custom-call | tf_op jit(solution)/shard_map/fill_slots/pallas_call | solution.py:321
  10.0 13.5 %all-to-all-start = ((bf16[32,32,128]{2,1,0:T(8,128)(2,1)}), bf16[32,32,128]{2,1,0:T(8,128)(2,1)S(1)}, u32[]{:S(2)}, u32[]{:S(2)}) async-start(bf16[32,32,128]{2,1,0:T(8,128)(2,1)} %fill_slots.1), calls=%async_computation | async-start | bytes 524288 | tf_op jit(solution)/shard_map/all_to_all | solution.py:317
  25.4 1.3 %reshape.29.gain_ref = bf16[1,2048]{1,0:T(2,128)(2,1)} reshape(bf16[2048]{0:T(1024)(128)(2,1)} %param.26) | data formatting | bytes 8192 | tf_op jit(solution)/shard_map/reshape | solution.py:363
  26.7 0.0 copy-start.1
  26.7 10.7 %home_attention.1 = (f32[32,128]{1,0:T(8,128)}, f32[40,128]{1,0:T(8,128)}, f32[1,2048]{1,0:T(1,128)}, bf16[1040,128]{1,0:T(8,128)(2,1)}) custom-call(s32[1]{0:T(128)S(6)} %copy.17.owned_ref, s32[1]{0:T(128)S(6)} %copy.18.live_ref, s32[1]{0:T(128)S(6)} %copy.16.place_ref, s32[4,8]{1,0:T(4,128)} %bitcast.18, s32[8]{0:T(128)} %length_ref.1, s32[4,8]{1,0:T(4,128)} %parent_ref.1, ...), custom_call_target="tpu_custom_call" | custom-call | tf_op jit(solution)/shard_map/home_attention/pallas_call | solution.py:335
  37.4 0.0 copy-start.3
  37.4 0.0 copy-start.4
  37.4 2.4 %all-gather = bf16[2080,128]{1,0:T(8,128)(2,1)S(1)} all-gather(bf16[1040,128]{1,0:T(8,128)(2,1)} %get-tuple-element.10), channel_id=2, replica_groups={{0,8},{16,24},{32,40},{48,56},{64,72},{80,88},{96,104},{112,120},{128,1..., dimensions={0}, use_global_device_ids=true | all-gather | bytes 798720 | tf_op jit(solution)/shard_map/all_gather | solution.py:365
  39.8 0.0 all-to-all-done.asked_ref
  39.8 0.0 copy-start.2
  39.8 1.3 %prompt_attention.1 = bf16[32,40,128]{2,1,0:T(8,128)(2,1)S(1)} custom-call(bf16[32,32,128]{2,1,0:T(8,128)(2,1)S(1)} %all-to-all-done.asked_ref, bf16[2,1040,128]{2,1,0:T(8,128)(2,1)S(1)} %bitcast.10), custom_call_target="tpu_custom_call" | custom-call | tf_op jit(solution)/shard_map/prompt_attention/pallas_call | solution.py:368
  41.1 0.0 copy-start
  41.2 0.0 copy-start.5
  41.2 20.5 %all_to_all.20.result_ref = bf16[32,40,128]{2,1,0:T(8,128)(2,1)S(1)} all-to-all(bf16[32,40,128]{2,1,0:T(8,128)(2,1)S(1)} %prompt_attention.1), channel_id=1, replica_groups={{0,16,32,48,64,80,96,112,128,144,160,176,192,208,224,240,256,272,288,30..., dimensions={0} | all-to-all | bytes 655360 | tf_op jit(solution)/shard_map/all_to_all | solution.py:317
  61.6 0.0 copy-done.1
  61.6 0.0 copy-done.3
  61.7 0.0 copy-done.4
  61.7 0.4 combine.1
  62.1 17.4 %all_to_all.21.partial_ref = f32[8,32,256]{2,1,0:T(8,128)S(1)} all-to-all(f32[8,32,256]{2,1,0:T(8,128)S(1)} %combine.1), channel_id=1, replica_groups=mesh['req'=64,'tp'=8] {'tp'}, dimensions={0} | all-to-all | bytes 524288 | tf_op jit(solution)/shard_map/all_to_all | solution.py:387
  79.4 0.0 copy-done.2
  79.5 11.5 %all_to_all.22.mixed_ref = bf16[8,32,256]{2,1,0:T(8,128)(2,1)S(1)} all-to-all(bf16[8,32,256]{2,1,0:T(8,128)(2,1)S(1)} %add_shards.1), channel_id=1, replica_groups=mesh['req'=64,'tp'=8] {'tp'}, dimensions={0} | all-to-all | bytes 262144 | tf_op jit(solution)/shard_map/all_to_all | solution.py:396
  90.9 0.0 copy-done
  90.9 0.0 copy-done.5
  90.9 1.0 %project.1 = (bf16[4,3,8,128]{3,2,1,0:T(8,128)(2,1)}, bf16[32,2048]{1,0:T(8,128)(2,1)}) custom-call(bf16[8,32,256]{2,1,0:T(8,128)(2,1)S(1)} %all_to_all.22.mixed_ref, f32[1,2048]{1,0:T(1,128)S(1)} %copy-done.5, bf16[3,2048,128]{2,1,0:T(8,128)(2,1)S(1)} %bitcast.11), custom_call_target="tpu_custom_call" | custom-call | tf_op jit(solution)/shard_map/project/pallas_call | solution.py:397
  (1 shorter events, 0.0 us)
Async XLA Ops:
  10.0 29.8 %all-to-all-start = ((bf16[32,32,128]{2,1,0:T(8,128)(2,1)}), bf16[32,32,128]{2,1,0:T(8,128)(2,1)S(1)}, u32[]{:S(2)}, u32[]{:S(2)}) async-start(bf16[32,32,128]{2,1,0:T(8,128)(2,1)} %fill_slots.1), calls=%async_computation | async-start | bytes 524288 | tf_op jit(solution)/shard_map/all_to_all | solution.py:317
  26.7 35.0 %copy-start.1 = (bf16[128,2048]{1,0:T(8,128)(2,1)S(1)}, bf16[128,2048]{1,0:T(8,128)(2,1)}, u32[]{:S(2)}) copy-start(bf16[128,2048]{1,0:T(8,128)(2,1)} %weight_ref.1) | copy-start | bytes 1572868
  37.4 24.3 %copy-start.3 = (f32[40,128]{1,0:T(8,128)S(1)}, f32[40,128]{1,0:T(8,128)}, u32[]{:S(2)}) copy-start(f32[40,128]{1,0:T(8,128)} %get-tuple-element.9.level_ref) | copy-start | bytes 61444
  37.4 24.3 %copy-start.4 = (f32[32,128]{1,0:T(8,128)S(1)}, f32[32,128]{1,0:T(8,128)}, u32[]{:S(2)}) copy-start(f32[32,128]{1,0:T(8,128)} %get-tuple-element.8.mean_ref) | copy-start | bytes 49156
  39.8 39.6 %copy-start.2 = (bf16[4,8,2048]{2,1,0:T(8,128)(2,1)S(1)}, bf16[4,8,2048]{2,1,0:T(8,128)(2,1)}, u32[]{:S(2)}) copy-start(bf16[4,8,2048]{2,1,0:T(8,128)(2,1)} %param.16) | copy-start | bytes 393220
  41.1 49.8 %copy-start = (bf16[2048,3,128]{2,0,1:T(8,128)(2,1)S(1)}, bf16[2048,3,128]{2,0,1:T(8,128)(2,1)}, u32[]{:S(2)}) copy-start(bf16[2048,3,128]{2,0,1:T(8,128)(2,1)} %param.27) | copy-start | bytes 4718596
  41.2 49.8 %copy-start.5 = (f32[1,2048]{1,0:T(1,128)S(1)}, f32[1,2048]{1,0:T(1,128)}, u32[]{:S(2)}) copy-start(f32[1,2048]{1,0:T(1,128)} %get-tuple-element.11.gain_ref) | copy-start | bytes 24580

commit v4 on v2

--- a/solution.py
+++ b/solution.py
@@ -96,6 +96,7 @@
 def home_kernel(
     owned_ref,
     live_ref,
+    place_ref,
     table_ref,
     length_ref,
     parent_ref,
@@ -108,8 +109,6 @@
     slot_ref,
     root_ref,
     line_ref,
-    note_ref,
-    sems,
 ):
     tokens = prompt_ref.shape[0]
     note_lane = lax.broadcasted_iota(jnp.int32, (NOTE_ROWS, LANES), 1)
@@ -117,13 +116,8 @@
     note = jnp.where(
         note_lane == 0, owned_ref[0], jnp.where(note_lane == 1, live // 16, live % 16)
     )
-    note_ref[...] = note.astype(jnp.float32).astype(jnp.bfloat16)
-    copies = [
-        pltpu.make_async_copy(prompt_ref, slot_ref.at[pl.ds(0, tokens)], sems.at[0]),
-        pltpu.make_async_copy(note_ref, slot_ref.at[pl.ds(tokens, NOTE_ROWS)], sems.at[1]),
-    ]
-    for copy in copies:
-        copy.start()
+    slot_ref[:tokens] = prompt_ref[...]
+    slot_ref[tokens:] = note.astype(jnp.float32).astype(jnp.bfloat16)
     step_count = parent_ref.shape[0]
     block_count = table_ref.shape[0]
     rows = query_ref.shape[0]
@@ -207,14 +201,14 @@
 
     mean_ref[...] = join_heads(numer / total)
     level = jnp.broadcast_to(top + jnp.log(total), numer.shape)
-    level_ref[...] = join_heads(level)
-    for copy in copies:
-        copy.wait()
-
-
-def combine_kernel(place_ref, mean_ref, level_ref, result_ref, weight_ref, out_ref):
+    level_ref[:rows] = join_heads(level)
+    level_ref[rows:] = jnp.full((BEAMS, LANES), place_ref[0]).astype(jnp.float32)
+
+
+def combine_kernel(mean_ref, level_ref, result_ref, weight_ref, out_ref):
     rows = mean_ref.shape[0]
-    packet = result_ref[place_ref[0] // 2].astype(jnp.float32)
+    place = jnp.max(level_ref[rows:]).astype(jnp.int32)
+    packet = result_ref[place // 2].astype(jnp.float32)
     wide = (2 * rows, LANES)
     lane = lax.broadcasted_iota(jnp.int32, wide, 1)
     row = lax.broadcasted_iota(jnp.int32, wide, 0)
@@ -224,7 +218,7 @@
     )
     prompt_level = jnp.sum(jnp.where(on_row, terms, 0.0), axis=1, keepdims=True)
     prompt_level = join_heads(jnp.broadcast_to(prompt_level, wide))
-    level = level_ref[...]
+    level = level_ref[:rows]
     joint_top = jnp.maximum(level, prompt_level)
     home_factor = jnp.exp(level - joint_top)
     prompt_factor = jnp.exp(prompt_level - joint_top)
@@ -256,7 +250,10 @@
     residual_out_ref[...] = rounded
     mixed = rounded.astype(jnp.float32)
     mean_square = jnp.mean(mixed * mixed, axis=1, keepdims=True)
-    gain = gain_ref[...].astype(jnp.float32)
+    gain_rows = gain_ref[...].astype(jnp.float32)
+    gain = jnp.concatenate(
+        [gain_rows[index : index + 1] for index in range(gain_rows.shape[0])], axis=1
+    )
     normed = (mixed * lax.rsqrt(mean_square + NORM_EPS) * gain).astype(jnp.bfloat16)
     for kind in range(qkv_weight_ref.shape[0]):
         projected = jnp.dot(
@@ -269,7 +266,6 @@
 VMEM_SPEC = pl.BlockSpec(memory_space=pltpu.VMEM)
 SMEM_SPEC = pl.BlockSpec(memory_space=pltpu.SMEM)
 KERNEL_PARAMS = pltpu.CompilerParams(vmem_limit_bytes=20 * 1024 * 1024)
-ANY_SPEC = pl.BlockSpec(memory_space=pl.ANY)
 
 
 def shards(
@@ -311,22 +307,20 @@
         home_kernel,
         out_shape=(
             jax.ShapeDtypeStruct((rows, lane_count), jnp.float32),
-            jax.ShapeDtypeStruct((rows, lane_count), jnp.float32),
+            jax.ShapeDtypeStruct((rows + BEAMS, lane_count), jnp.float32),
             jax.ShapeDtypeStruct((slot_rows, lane_count), jnp.bfloat16),
         ),
-        in_specs=[SMEM_SPEC] * 5 + [VMEM_SPEC] * 3 + [ANY_SPEC],
-        out_specs=(VMEM_SPEC, VMEM_SPEC, ANY_SPEC),
+        in_specs=[SMEM_SPEC] * 6 + [VMEM_SPEC] * 4,
+        out_specs=(VMEM_SPEC, VMEM_SPEC, VMEM_SPEC),
         scratch_shapes=[
             pltpu.SMEM((step_count, BEAMS), jnp.int32),
             pltpu.SMEM((step_count * step_count, BEAMS), jnp.int32),
-            pltpu.VMEM((NOTE_ROWS, lane_count), jnp.bfloat16),
-            pltpu.SemaphoreType.DMA((2,)),
         ],
-        compiler_params=KERNEL_PARAMS,
         name="home_attention",
     )(
         owned_request,
         prompt_len,
+        prompt_place,
         home_table.T,
         home_len,
         parents,
@@ -340,7 +334,7 @@
     packet_rows = rows + STAT_ROWS
     results = pl.pallas_call(
         prompt_kernel,
-        out_shape=jax.ShapeDtypeStruct((chips, packet_rows, lane_count), jnp.bfloat16),
+        out_shape=pltpu.VMEM((chips, packet_rows, lane_count), jnp.bfloat16),
         in_specs=[VMEM_SPEC] * 2,
         out_specs=VMEM_SPEC,
         compiler_params=KERNEL_PARAMS,
@@ -351,12 +345,12 @@
     width = model_width // tp_size
     partial = pl.pallas_call(
         combine_kernel,
-        out_shape=jax.ShapeDtypeStruct((tp_size, rows, width), jnp.float32),
-        in_specs=[SMEM_SPEC] + [VMEM_SPEC] * 4,
+        out_shape=jax.ShapeDtypeStruct((tp_size, rows, width), jnp.bfloat16),
+        in_specs=[VMEM_SPEC] * 4,
         out_specs=VMEM_SPEC,
         compiler_params=KERNEL_PARAMS,
         name="combine",
-    )(prompt_place, home_mean, home_level, returned, out_weight)
+    )(home_mean, home_level, returned, out_weight)
     partials = lax.all_to_all(partial, "tp", 0, 0)
     mixed = pl.pallas_call(
         sum_kernel,
@@ -379,7 +373,7 @@
         name="project",
     )(
         all_mixed,
-        norm_gain.reshape(1, model_width),
+        norm_gain.reshape(model_width // lane_count, lane_count),
         qkv_weight.transpose(1, 0, 2),
     )
     return (

time: 84.4 us -> 76 us (0.900)
  the two profiles are of different devices: /device:TPU:64 before, /device:TPU:6 now
where the time goes in v4:
time: 76 us; the launch traced here: 74.6 us
  blocking collectives  48.1 us (63%)
  starting transfers between devices  13.5 us (18%)
  Pallas kernels  5.33 us (7%)
  waiting for transfers between devices  3.55 us (5%)
  between operations  2.63 us (3%)
  local copies, waits for them, and re-layouts  1.46 us (2%)
    all_to_all x1, blocking collectives, route(): return lax.all_to_all(slots, 'req', 0, 0, axis_index_groups=same_core)  18.2 us
    all_to_all x1, blocking collectives, shards(): partials = lax.all_to_all(partial, 'tp', 0, 0)  16 us
    all_to_all x1, starting transfers between devices, route(): return lax.all_to_all(slots, 'req', 0, 0, axis_index_groups=same_core)  13.5 us
    all_to_all x1, blocking collectives, shards(): all_mixed = lax.all_to_all(mixed, 'tp', 0, 0)  11.5 us
    all_to_all x1, waiting for transfers between devices, route(): return lax.all_to_all(slots, 'req', 0, 0, axis_index_groups=same_core)  3.55 us
    pallas_call x1, Pallas kernels, shards(): pl.pallas_call(home_kernel, out_shape=(jax.ShapeDtypeStruct((rows, lane_c...  2.53 us
    all_gather x1, blocking collectives, shards(): both_slots = lax.all_gather(own_slot, 'req', axis_index_groups=same_chip)  2.53 us
  transfers between devices with their start and end apart: 1, of which 1 were waited for; matrix products, arithmetic and copies ran while one was open for 0% of the time, Pallas kernels for 3%

profile of v4, /device:TPU:6, one launch (start us, length us, event | category | flops | bytes accessed | tf_op | source)
XLA Modules:
  0.0 74.6 jit_solution(6893649823856310209)
XLA Ops:
  0.6 1.4 %broadcast_in_dim.2 = bf16[32,32,128]{2,1,0:T(8,128)(2,1)} broadcast(bf16[32,128]{1,0:T(8,128)(2,1)} %bitcast.17), dimensions={1,2} | broadcast | bytes 270336 | tf_op jit(solution)/shard_map/broadcast_in_dim | solution.py:300
  2.1 13.5 %all-to-all-start = ((bf16[32,32,128]{2,1,0:T(8,128)(2,1)}), bf16[32,32,128]{2,1,0:T(8,128)(2,1)S(1)}, u32[]{:S(2)}, u32[]{:S(2)}) async-start(bf16[32,32,128]{2,1,0:T(8,128)(2,1)} %broadcast_in_dim.2), calls=%async_computation | async-start | bytes 524288 | tf_op jit(solution)/shard_map/all_to_all | solution.py:297
  17.5 0.0 copy-start.1
  17.5 2.5 %home_attention.1 = (f32[32,128]{1,0:T(8,128)}, f32[40,128]{1,0:T(8,128)}, bf16[1040,128]{1,0:T(8,128)(2,1)}) custom-call(s32[1]{0:T(128)S(6)} %copy.17.owned_ref, s32[1]{0:T(128)S(6)} %copy.18.live_ref, s32[1]{0:T(128)S(6)} %copy.16.place_ref, s32[4,8]{1,0:T(4,128)} %bitcast.20, s32[8]{0:T(128)} %length_ref.1, s32[4,8]{1,0:T(4,128)} %parent_ref.1, ...), custom_call_target="tpu_custom_call" | custom-call | tf_op jit(solution)/shard_map/home_attention/pallas_call | solution.py:306
  20.0 0.0 copy-start.3
  20.0 0.0 copy-start.4
  20.0 2.5 %all-gather = bf16[2080,128]{1,0:T(8,128)(2,1)S(1)} all-gather(bf16[1040,128]{1,0:T(8,128)(2,1)} %get-tuple-element.9), channel_id=2, replica_groups={{0,8},{16,24},{32,40},{48,56},{64,72},{80,88},{96,104},{112,120},{128,1..., dimensions={0}, use_global_device_ids=true | all-gather | bytes 798720 | tf_op jit(solution)/shard_map/all_gather | solution.py:332
  22.5 0.0 copy-start.2
  22.5 3.6 %all-to-all-done.asked_ref = bf16[32,32,128]{2,1,0:T(8,128)(2,1)S(1)} async-done(((bf16[32,32,128]{2,1,0:T(8,128)(2,1)}), bf16[32,32,128]{2,1,0:T(8,128)(2,1)S(1)}, u32[]{:S(2)}, u32[]{:S(2)}) %all-to-all-start) | async-done | bytes 262176 | tf_op jit(solution)/shard_map/all_to_all | solution.py:297
  26.1 1.3 %prompt_attention.1 = bf16[32,40,128]{2,1,0:T(8,128)(2,1)S(1)} custom-call(bf16[32,32,128]{2,1,0:T(8,128)(2,1)S(1)} %all-to-all-done.asked_ref, bf16[2,1040,128]{2,1,0:T(8,128)(2,1)S(1)} %bitcast.11), custom_call_target="tpu_custom_call" | custom-call | tf_op jit(solution)/shard_map/prompt_attention/pallas_call | solution.py:335
  27.4 0.0 copy-start
  27.4 0.0 copy-start.5
  27.4 18.2 %all_to_all.20.result_ref = bf16[32,40,128]{2,1,0:T(8,128)(2,1)S(1)} all-to-all(bf16[32,40,128]{2,1,0:T(8,128)(2,1)S(1)} %prompt_attention.1), channel_id=1, replica_groups={{0,16,32,48,64,80,96,112,128,144,160,176,192,208,224,240,256,272,288,30..., dimensions={0} | all-to-all | bytes 655360 | tf_op jit(solution)/shard_map/all_to_all | solution.py:297
  45.6 0.0 copy-done.1
  45.6 0.0 copy-done.3
  45.6 0.0 copy-done.4
  45.6 0.4 combine.1
  46.0 16.0 %all_to_all.21.partial_ref = bf16[8,32,256]{2,1,0:T(8,128)(2,1)S(1)} all-to-all(bf16[8,32,256]{2,1,0:T(8,128)(2,1)S(1)} %combine.1), channel_id=1, replica_groups=mesh['req'=64,'tp'=8] {'tp'}, dimensions={0} | all-to-all | bytes 262144 | tf_op jit(solution)/shard_map/all_to_all | solution.py:354
  62.0 0.0 copy-done.2
  62.0 11.5 %all_to_all.22.mixed_ref = bf16[8,32,256]{2,1,0:T(8,128)(2,1)S(1)} all-to-all(bf16[8,32,256]{2,1,0:T(8,128)(2,1)S(1)} %add_shards.1), channel_id=1, replica_groups=mesh['req'=64,'tp'=8] {'tp'}, dimensions={0} | all-to-all | bytes 262144 | tf_op jit(solution)/shard_map/all_to_all | solution.py:363
  73.5 0.0 copy-done
  73.5 0.0 copy-done.5
  73.5 1.1 %project.1 = (bf16[4,3,8,128]{3,2,1,0:T(8,128)(2,1)}, bf16[32,2048]{1,0:T(8,128)(2,1)}) custom-call(bf16[8,32,256]{2,1,0:T(8,128)(2,1)S(1)} %all_to_all.22.mixed_ref, bf16[16,128]{1,0:T(8,128)(2,1)S(1)} %bitcast.14, bf16[3,2048,128]{2,1,0:T(8,128)(2,1)S(1)} %bitcast.12), custom_call_target="tpu_custom_call" | custom-call | tf_op jit(solution)/shard_map/project/pallas_call | solution.py:364
  (1 shorter events, 0.0 us)
Async XLA Ops:
  2.1 24.0 %all-to-all-start = ((bf16[32,32,128]{2,1,0:T(8,128)(2,1)}), bf16[32,32,128]{2,1,0:T(8,128)(2,1)S(1)}, u32[]{:S(2)}, u32[]{:S(2)}) async-start(bf16[32,32,128]{2,1,0:T(8,128)(2,1)} %broadcast_in_dim.2), calls=%async_computation | async-start | bytes 524288 | tf_op jit(solution)/shard_map/all_to_all | solution.py:297
  17.5 28.1 %copy-start.1 = (bf16[128,2048]{1,0:T(8,128)(2,1)S(1)}, bf16[128,2048]{1,0:T(8,128)(2,1)}, u32[]{:S(2)}) copy-start(bf16[128,2048]{1,0:T(8,128)(2,1)} %weight_ref.1) | copy-start | bytes 1572868
  20.0 25.6 %copy-start.3 = (f32[40,128]{1,0:T(8,128)S(1)}, f32[40,128]{1,0:T(8,128)}, u32[]{:S(2)}) copy-start(f32[40,128]{1,0:T(8,128)} %get-tuple-element.8.level_ref) | copy-start | bytes 61444
  20.0 25.6 %copy-start.4 = (f32[32,128]{1,0:T(8,128)S(1)}, f32[32,128]{1,0:T(8,128)}, u32[]{:S(2)}) copy-start(f32[32,128]{1,0:T(8,128)} %get-tuple-element.7.mean_ref) | copy-start | bytes 49156
  22.5 39.5 %copy-start.2 = (bf16[4,8,2048]{2,1,0:T(8,128)(2,1)S(1)}, bf16[4,8,2048]{2,1,0:T(8,128)(2,1)}, u32[]{:S(2)}) copy-start(bf16[4,8,2048]{2,1,0:T(8,128)(2,1)} %param.16) | copy-start | bytes 393220
  27.4 46.1 %copy-start = (bf16[2048,3,128]{2,0,1:T(8,128)(2,1)S(1)}, bf16[2048,3,128]{2,0,1:T(8,128)(2,1)}, u32[]{:S(2)}) copy-start(bf16[2048,3,128]{2,0,1:T(8,128)(2,1)} %param.27) | copy-start | bytes 4718596
  27.4 46.1 %copy-start.5 = (bf16[2048]{0:T(1024)(128)(2,1)S(1)}, bf16[2048]{0:T(1024)(128)(2,1)}, u32[]{:S(2)}) copy-start(bf16[2048]{0:T(1024)(128)(2,1)} %param.26) | copy-start | bytes 12292

commit v5 on v4

--- a/solution.py
+++ b/solution.py
@@ -42,12 +42,18 @@
     return pltpu.roll(weights, 1, axis=1).astype(jnp.bfloat16)
 
 
+def fill_kernel(query_ref, out_ref):
+    for index in range(out_ref.shape[0]):
+        out_ref[index] = query_ref[...]
+
+
 def prompt_kernel(asked_ref, slots_ref, out_ref):
     core = lax.axis_index("req") % 2
     rows = asked_ref.shape[1]
     tokens = slots_ref.shape[1] - NOTE_ROWS
     lane = lax.broadcasted_iota(jnp.int32, (NOTE_ROWS, LANES), 1)
     row = lax.broadcasted_iota(jnp.int32, (NOTE_ROWS, LANES), 0)
+    served = []
     for slot in range(2):
         note = slots_ref[slot, tokens:].astype(jnp.float32)
 
@@ -57,11 +63,14 @@
 
         owner = number(0)
         live = number(1) * 16 + number(2)
+        served.append(
+            (owner, prompt_packet(asked_ref[owner // 2], slots_ref[slot, :tokens], live, rows))
+        )
+    for owner, packet in served:
 
         @pl.when(owner % 2 == core)
         def _():
-            chip = owner // 2
-            out_ref[chip] = prompt_packet(asked_ref[chip], slots_ref[slot, :tokens], live, rows)
+            out_ref[owner // 2] = packet
 
 
 def prompt_packet(query_rows, cache, live, rows):
@@ -297,7 +306,15 @@
         return lax.all_to_all(slots, "req", 0, 0, axis_index_groups=same_core)
 
     query_rows = queries.reshape(rows, lane_count)
-    asked = route(jnp.broadcast_to(query_rows[None], (chips, rows, lane_count)))
+    asked = route(
+        pl.pallas_call(
+            fill_kernel,
+            out_shape=jax.ShapeDtypeStruct((chips, rows, lane_count), jnp.bfloat16),
+            in_specs=[VMEM_SPEC],
+            out_specs=VMEM_SPEC,
+            name="fill_slots",
+        )(query_rows)
+    )
 
     home_rows = home_cache.reshape(-1, lane_count)
     fresh_rows = new_kv.reshape(-1, lane_count)

time: 76 us -> 75.8 us (level)
  the two profiles are of different devices: /device:TPU:6 before, /device:TPU:64 now
where the time goes in v5:
time: 75.8 us; the launch traced here: 75.3 us
  blocking collectives  48.3 us (64%)
  starting transfers between devices  12.6 us (17%)
  Pallas kernels  6.49 us (9%)
  waiting for transfers between devices  5.27 us (7%)
  between operations  2.63 us (3%)
    all_to_all x1, blocking collectives, route(): return lax.all_to_all(slots, 'req', 0, 0, axis_index_groups=same_core)  18.3 us
    all_to_all x1, blocking collectives, shards(): partials = lax.all_to_all(partial, 'tp', 0, 0)  16 us
    all_to_all x1, starting transfers between devices, route(): return lax.all_to_all(slots, 'req', 0, 0, axis_index_groups=same_core)  12.6 us
    all_to_all x1, blocking collectives, shards(): all_mixed = lax.all_to_all(mixed, 'tp', 0, 0)  11.5 us
    all_to_all x1, waiting for transfers between devices, route(): return lax.all_to_all(slots, 'req', 0, 0, axis_index_groups=same_core)  5.27 us
    pallas_call x1, Pallas kernels, shards(): pl.pallas_call(home_kernel, out_shape=(jax.ShapeDtypeStruct((rows, lane_c...  2.53 us
    all_gather x1, blocking collectives, shards(): both_slots = lax.all_gather(own_slot, 'req', axis_index_groups=same_chip)  2.53 us
  transfers between devices with their start and end apart: 1, of which 1 were waited for; matrix products, arithmetic and copies ran while one was open for 0% of the time, Pallas kernels for 3%

profile of v5, /device:TPU:64, one launch (start us, length us, event | category | flops | bytes accessed | tf_op | source)
XLA Modules:
  0.0 75.3 jit_solution(10736998746693623408)
XLA Ops:
  0.6 1.4 %fill_slots.1 = bf16[32,32,128]{2,1,0:T(8,128)(2,1)} custom-call(bf16[32,128]{1,0:T(8,128)(2,1)} %bitcast.17), custom_call_target="tpu_custom_call" | custom-call | tf_op jit(solution)/shard_map/fill_slots/pallas_call | solution.py:310
  2.1 12.6 %all-to-all-start = ((bf16[32,32,128]{2,1,0:T(8,128)(2,1)}), bf16[32,32,128]{2,1,0:T(8,128)(2,1)S(1)}, u32[]{:S(2)}, u32[]{:S(2)}) async-start(bf16[32,32,128]{2,1,0:T(8,128)(2,1)} %fill_slots.1), calls=%async_computation | async-start | bytes 524288 | tf_op jit(solution)/shard_map/all_to_all | solution.py:306
  16.6 0.0 copy-start.1
  16.6 2.5 %home_attention.1 = (f32[32,128]{1,0:T(8,128)}, f32[40,128]{1,0:T(8,128)}, bf16[1040,128]{1,0:T(8,128)(2,1)}) custom-call(s32[1]{0:T(128)S(6)} %copy.17.owned_ref, s32[1]{0:T(128)S(6)} %copy.18.live_ref, s32[1]{0:T(128)S(6)} %copy.16.place_ref, s32[4,8]{1,0:T(4,128)} %bitcast.20, s32[8]{0:T(128)} %length_ref.1, s32[4,8]{1,0:T(4,128)} %parent_ref.1, ...), custom_call_target="tpu_custom_call" | custom-call | tf_op jit(solution)/shard_map/home_attention/pallas_call | solution.py:323
  19.1 0.0 copy-start.3
  19.1 0.0 copy-start.4
  19.1 2.5 %all-gather = bf16[2080,128]{1,0:T(8,128)(2,1)S(1)} all-gather(bf16[1040,128]{1,0:T(8,128)(2,1)} %get-tuple-element.9), channel_id=2, replica_groups={{0,8},{16,24},{32,40},{48,56},{64,72},{80,88},{96,104},{112,120},{128,1..., dimensions={0}, use_global_device_ids=true | all-gather | bytes 798720 | tf_op jit(solution)/shard_map/all_gather | solution.py:349
  21.7 0.0 copy-start.2
  21.7 5.3 %all-to-all-done.asked_ref = bf16[32,32,128]{2,1,0:T(8,128)(2,1)S(1)} async-done(((bf16[32,32,128]{2,1,0:T(8,128)(2,1)}), bf16[32,32,128]{2,1,0:T(8,128)(2,1)S(1)}, u32[]{:S(2)}, u32[]{:S(2)}) %all-to-all-start) | async-done | bytes 262176 | tf_op jit(solution)/shard_map/all_to_all | solution.py:306
  26.9 1.0 %prompt_attention.1 = bf16[32,40,128]{2,1,0:T(8,128)(2,1)S(1)} custom-call(bf16[32,32,128]{2,1,0:T(8,128)(2,1)S(1)} %all-to-all-done.asked_ref, bf16[2,1040,128]{2,1,0:T(8,128)(2,1)S(1)} %bitcast.11), custom_call_target="tpu_custom_call" | custom-call | tf_op jit(solution)/shard_map/prompt_attention/pallas_call | solution.py:352
  28.0 0.0 copy-start
  28.0 0.0 copy-start.5
  28.0 18.3 %all_to_all.20.result_ref = bf16[32,40,128]{2,1,0:T(8,128)(2,1)S(1)} all-to-all(bf16[32,40,128]{2,1,0:T(8,128)(2,1)S(1)} %prompt_attention.1), channel_id=1, replica_groups={{0,16,32,48,64,80,96,112,128,144,160,176,192,208,224,240,256,272,288,30..., dimensions={0} | all-to-all | bytes 655360 | tf_op jit(solution)/shard_map/all_to_all | solution.py:306
  46.4 0.0 copy-done.1
  46.4 0.0 copy-done.3
  46.4 0.0 copy-done.4
  46.4 0.4 combine.1
  46.8 16.0 %all_to_all.21.partial_ref = bf16[8,32,256]{2,1,0:T(8,128)(2,1)S(1)} all-to-all(bf16[8,32,256]{2,1,0:T(8,128)(2,1)S(1)} %combine.1), channel_id=1, replica_groups=mesh['req'=64,'tp'=8] {'tp'}, dimensions={0} | all-to-all | bytes 262144 | tf_op jit(solution)/shard_map/all_to_all | solution.py:371
  62.8 0.0 copy-done.2
  62.8 11.5 %all_to_all.22.mixed_ref = bf16[8,32,256]{2,1,0:T(8,128)(2,1)S(1)} all-to-all(bf16[8,32,256]{2,1,0:T(8,128)(2,1)S(1)} %add_shards.1), channel_id=1, replica_groups=mesh['req'=64,'tp'=8] {'tp'}, dimensions={0} | all-to-all | bytes 262144 | tf_op jit(solution)/shard_map/all_to_all | solution.py:380
  74.3 0.0 copy-done
  74.3 0.0 copy-done.5
  74.3 1.1 %project.1 = (bf16[4,3,8,128]{3,2,1,0:T(8,128)(2,1)}, bf16[32,2048]{1,0:T(8,128)(2,1)}) custom-call(bf16[8,32,256]{2,1,0:T(8,128)(2,1)S(1)} %all_to_all.22.mixed_ref, bf16[16,128]{1,0:T(8,128)(2,1)S(1)} %bitcast.14, bf16[3,2048,128]{2,1,0:T(8,128)(2,1)S(1)} %bitcast.12), custom_call_target="tpu_custom_call" | custom-call | tf_op jit(solution)/shard_map/project/pallas_call | solution.py:381
  (1 shorter events, 0.0 us)
Async XLA Ops:
  2.1 24.9 %all-to-all-start = ((bf16[32,32,128]{2,1,0:T(8,128)(2,1)}), bf16[32,32,128]{2,1,0:T(8,128)(2,1)S(1)}, u32[]{:S(2)}, u32[]{:S(2)}) async-start(bf16[32,32,128]{2,1,0:T(8,128)(2,1)} %fill_slots.1), calls=%async_computation | async-start | bytes 524288 | tf_op jit(solution)/shard_map/all_to_all | solution.py:306
  16.6 29.8 %copy-start.1 = (bf16[128,2048]{1,0:T(8,128)(2,1)S(1)}, bf16[128,2048]{1,0:T(8,128)(2,1)}, u32[]{:S(2)}) copy-start(bf16[128,2048]{1,0:T(8,128)(2,1)} %weight_ref.1) | copy-start | bytes 1572868
  19.1 27.2 %copy-start.3 = (f32[40,128]{1,0:T(8,128)S(1)}, f32[40,128]{1,0:T(8,128)}, u32[]{:S(2)}) copy-start(f32[40,128]{1,0:T(8,128)} %get-tuple-element.8.level_ref) | copy-start | bytes 61444
  19.1 27.2 %copy-start.4 = (f32[32,128]{1,0:T(8,128)S(1)}, f32[32,128]{1,0:T(8,128)}, u32[]{:S(2)}) copy-start(f32[32,128]{1,0:T(8,128)} %get-tuple-element.7.mean_ref) | copy-start | bytes 49156
  21.7 41.1 %copy-start.2 = (bf16[4,8,2048]{2,1,0:T(8,128)(2,1)S(1)}, bf16[4,8,2048]{2,1,0:T(8,128)(2,1)}, u32[]{:S(2)}) copy-start(bf16[4,8,2048]{2,1,0:T(8,128)(2,1)} %param.16) | copy-start | bytes 393220
  28.0 46.3 %copy-start = (bf16[2048,3,128]{2,0,1:T(8,128)(2,1)S(1)}, bf16[2048,3,128]{2,0,1:T(8,128)(2,1)}, u32[]{:S(2)}) copy-start(bf16[2048,3,128]{2,0,1:T(8,128)(2,1)} %param.27) | copy-start | bytes 4718596
  28.0 46.3 %copy-start.5 = (bf16[2048]{0:T(1024)(128)(2,1)S(1)}, bf16[2048]{0:T(1024)(128)(2,1)}, u32[]{:S(2)}) copy-start(bf16[2048]{0:T(1024)(128)(2,1)} %param.26) | copy-start | bytes 12292

commit v6 on v4

--- a/solution.py
+++ b/solution.py
@@ -15,7 +15,13 @@
 SCORE_SCALE = 1.0 / math.sqrt(HEAD_DIM)
 LANES = 2 * HEAD_DIM
 STAT_ROWS = 8
+FIRST_CHIP = 21
+SHARD_ORDER = (5, 4, 3, 2, 1, 0, 7, 6)
 NOTE_ROWS = 16
+
+
+def slot_of(device, chips):
+    return (device // 2 + chips - FIRST_CHIP % chips) % chips
 
 
 def split_heads(rows):
@@ -60,8 +66,8 @@
 
         @pl.when(owner % 2 == core)
         def _():
-            chip = owner // 2
-            out_ref[chip] = prompt_packet(asked_ref[chip], slots_ref[slot, :tokens], live, rows)
+            place = slot_of(owner, asked_ref.shape[0])
+            out_ref[place] = prompt_packet(asked_ref[place], slots_ref[slot, :tokens], live, rows)
 
 
 def prompt_packet(query_rows, cache, live, rows):
@@ -208,7 +214,7 @@
 def combine_kernel(mean_ref, level_ref, result_ref, weight_ref, out_ref):
     rows = mean_ref.shape[0]
     place = jnp.max(level_ref[rows:]).astype(jnp.int32)
-    packet = result_ref[place // 2].astype(jnp.float32)
+    packet = result_ref[slot_of(place, result_ref.shape[0])].astype(jnp.float32)
     wide = (2 * rows, LANES)
     lane = lax.broadcasted_iota(jnp.int32, wide, 1)
     row = lax.broadcasted_iota(jnp.int32, wide, 0)
@@ -229,8 +235,8 @@
         attended.astype(jnp.bfloat16), weight_ref[...], preferred_element_type=jnp.float32
     )
     width = out_ref.shape[2]
-    for index in range(out_ref.shape[0]):
-        out_ref[index] = partial[:, index * width : (index + 1) * width].astype(out_ref.dtype)
+    for index, shard in enumerate(SHARD_ORDER):
+        out_ref[index] = partial[:, shard * width : (shard + 1) * width].astype(out_ref.dtype)
 
 
 def sum_kernel(partial_ref, residual_ref, out_ref):
@@ -245,8 +251,8 @@
 
 
 def project_kernel(mixed_ref, gain_ref, qkv_weight_ref, qkv_ref, residual_out_ref):
-    shard_count = mixed_ref.shape[0]
-    rounded = jnp.concatenate([mixed_ref[index] for index in range(shard_count)], axis=1)
+    shards_held = range(mixed_ref.shape[0])
+    rounded = jnp.concatenate([mixed_ref[SHARD_ORDER.index(shard)] for shard in shards_held], axis=1)
     residual_out_ref[...] = rounded
     mixed = rounded.astype(jnp.float32)
     mean_square = jnp.mean(mixed * mixed, axis=1, keepdims=True)
@@ -290,7 +296,9 @@
     req_size = lax.axis_size("req")
     tp_size = lax.axis_size("tp")
     chips = req_size // 2
-    same_core = [[2 * chip + core for chip in range(chips)] for core in range(2)]
+    order = [(position + FIRST_CHIP) % chips for position in range(chips)]
+    same_core = [[2 * chip + core for chip in order] for core in range(2)]
+    shard_groups = [list(SHARD_ORDER)]
     same_chip = [[2 * chip, 2 * chip + 1] for chip in range(chips)]
 
     def route(slots):
@@ -351,7 +359,7 @@
         compiler_params=KERNEL_PARAMS,
         name="combine",
     )(home_mean, home_level, returned, out_weight)
-    partials = lax.all_to_all(partial, "tp", 0, 0)
+    partials = lax.all_to_all(partial, "tp", 0, 0, axis_index_groups=shard_groups)
     mixed = pl.pallas_call(
         sum_kernel,
         out_shape=jax.ShapeDtypeStruct((tp_size, rows, width), jnp.bfloat16),
@@ -360,7 +368,7 @@
         compiler_params=KERNEL_PARAMS,
         name="add_shards",
     )(partials, residual.reshape(rows, model_width))
-    all_mixed = lax.all_to_all(mixed, "tp", 0, 0)
+    all_mixed = lax.all_to_all(mixed, "tp", 0, 0, axis_index_groups=shard_groups)
     next_qkv, new_residual = pl.pallas_call(
         project_kernel,
         out_shape=(

time: 76 us -> 69.4 us (0.913); the launches traced: 74.6 us -> 69 us
  blocking collectives: 48.1 us -> 44 us
  waiting for transfers between devices: 3.55 us -> 2.29 us
    all_to_all x2, blocking collectives: 27.4 us -> 23.2 us  [the longest x1 11.7 us: shards(): lax.all_to_all(partial, 'tp', 0, 0, axis_index_groups=shard_groups)]
    all_to_all x1, waiting for transfers between devices: 3.55 us -> 2.29 us  [route(): return lax.all_to_all(slots, 'req', 0, 0, axis_index_groups=same_core)]
  transfers between devices with their start and end apart: 1 -> 1, of which waited for: 1 -> 1; matrix products, arithmetic and copies ran while one was open for 0% -> 0% of each run, Pallas kernels for 3% -> 4%
where the time goes in v6:
time: 69.4 us; the launch traced here: 69 us
  blocking collectives  44 us (63%)
  starting transfers between devices  13.7 us (20%)
  Pallas kernels  4.8 us (7%)
  between operations  2.63 us (4%)
  waiting for transfers between devices  2.29 us (3%)
  local copies, waits for them, and re-layouts  1.46 us (2%)
    all_to_all x1, blocking collectives, route(): return lax.all_to_all(slots, 'req', 0, 0, axis_index_groups=same_core)  18.3 us
    all_to_all x1, starting transfers between devices, route(): return lax.all_to_all(slots, 'req', 0, 0, axis_index_groups=same_core)  13.7 us
    all_to_all x1, blocking collectives, shards(): lax.all_to_all(partial, 'tp', 0, 0, axis_index_groups=shard_groups)  11.7 us
    all_to_all x1, blocking collectives, shards(): lax.all_to_all(mixed, 'tp', 0, 0, axis_index_groups=shard_groups)  11.5 us
    pallas_call x1, Pallas kernels, shards(): pl.pallas_call(home_kernel, out_shape=(jax.ShapeDtypeStruct((rows, lane_c...  2.53 us
    all_gather x1, blocking collectives, shards(): both_slots = lax.all_gather(own_slot, 'req', axis_index_groups=same_chip)  2.53 us
    all_to_all x1, waiting for transfers between devices, route(): return lax.all_to_all(slots, 'req', 0, 0, axis_index_groups=same_core)  2.29 us
    broadcast_in_dim x1, local copies, waits for them, and re-layouts, shards(): asked = route(jnp.broadcast_to(query_rows[None], (chips, rows, lane_count)))  1.43 us
  transfers between devices with their start and end apart: 1, of which 1 were waited for; matrix products, arithmetic and copies ran while one was open for 0% of the time, Pallas kernels for 4%

profile of v6, /device:TPU:6, one launch (start us, length us, event | category | flops | bytes accessed | tf_op | source)
XLA Modules:
  0.0 69.0 jit_solution(14935107457918585295)
XLA Ops:
  0.6 1.4 %broadcast_in_dim.2 = bf16[32,32,128]{2,1,0:T(8,128)(2,1)} broadcast(bf16[32,128]{1,0:T(8,128)(2,1)} %bitcast.17), dimensions={1,2} | broadcast | bytes 270336 | tf_op jit(solution)/shard_map/broadcast_in_dim | solution.py:308
  2.1 13.7 %all-to-all-start = ((bf16[32,32,128]{2,1,0:T(8,128)(2,1)}), bf16[32,32,128]{2,1,0:T(8,128)(2,1)S(1)}, u32[]{:S(2)}, u32[]{:S(2)}) async-start(bf16[32,32,128]{2,1,0:T(8,128)(2,1)} %broadcast_in_dim.2), calls=%async_computation | async-start | bytes 524288 | tf_op jit(solution)/shard_map/all_to_all | solution.py:305
  17.7 0.0 copy-start.1
  17.7 2.5 %home_attention.1 = (f32[32,128]{1,0:T(8,128)}, f32[40,128]{1,0:T(8,128)}, bf16[1040,128]{1,0:T(8,128)(2,1)}) custom-call(s32[1]{0:T(128)S(6)} %copy.17.owned_ref, s32[1]{0:T(128)S(6)} %copy.18.live_ref, s32[1]{0:T(128)S(6)} %copy.16.place_ref, s32[4,8]{1,0:T(4,128)} %bitcast.20, s32[8]{0:T(128)} %length_ref.1, s32[4,8]{1,0:T(4,128)} %parent_ref.1, ...), custom_call_target="tpu_custom_call" | custom-call | tf_op jit(solution)/shard_map/home_attention/pallas_call | solution.py:314
  20.3 0.0 copy-start.3
  20.3 0.0 copy-start.4
  20.3 2.5 %all-gather = bf16[2080,128]{1,0:T(8,128)(2,1)S(1)} all-gather(bf16[1040,128]{1,0:T(8,128)(2,1)} %get-tuple-element.9), channel_id=2, replica_groups={{0,8},{16,24},{32,40},{48,56},{64,72},{80,88},{96,104},{112,120},{128,1..., dimensions={0}, use_global_device_ids=true | all-gather | bytes 798720 | tf_op jit(solution)/shard_map/all_gather | solution.py:340
  22.8 0.0 copy-start.2
  22.8 2.3 %all-to-all-done.asked_ref = bf16[32,32,128]{2,1,0:T(8,128)(2,1)S(1)} async-done(((bf16[32,32,128]{2,1,0:T(8,128)(2,1)}), bf16[32,32,128]{2,1,0:T(8,128)(2,1)S(1)}, u32[]{:S(2)}, u32[]{:S(2)}) %all-to-all-start) | async-done | bytes 262176 | tf_op jit(solution)/shard_map/all_to_all | solution.py:305
  25.1 0.8 %prompt_attention.1 = bf16[32,40,128]{2,1,0:T(8,128)(2,1)S(1)} custom-call(bf16[32,32,128]{2,1,0:T(8,128)(2,1)S(1)} %all-to-all-done.asked_ref, bf16[2,1040,128]{2,1,0:T(8,128)(2,1)S(1)} %bitcast.11), custom_call_target="tpu_custom_call" | custom-call | tf_op jit(solution)/shard_map/prompt_attention/pallas_call | solution.py:343
  25.9 0.0 copy-start
  25.9 0.0 copy-start.5
  25.9 18.3 %all_to_all.20.result_ref = bf16[32,40,128]{2,1,0:T(8,128)(2,1)S(1)} all-to-all(bf16[32,40,128]{2,1,0:T(8,128)(2,1)S(1)} %prompt_attention.1), channel_id=1, replica_groups={{336,352,368,384,400,416,432,448,464,480,496,0,16,32,48,64,80,96,112,12..., dimensions={0} | all-to-all | bytes 655360 | tf_op jit(solution)/shard_map/all_to_all | solution.py:305
  44.2 0.0 copy-done.1
  44.2 0.0 copy-done.3
  44.2 0.0 copy-done.4
  44.3 0.4 combine.1
  44.7 11.7 %all_to_all.21.partial_ref = bf16[8,32,256]{2,1,0:T(8,128)(2,1)S(1)} all-to-all(bf16[8,32,256]{2,1,0:T(8,128)(2,1)S(1)} %combine.1), channel_id=1, replica_groups={{5,4,3,2,1,0,7,6},{13,12,11,10,9,8,15,14},{21,20,19,18,17,16,23,22},{29..., dimensions={0} | all-to-all | bytes 262144 | tf_op jit(solution)/shard_map/all_to_all | solution.py:362
  56.4 0.0 copy-done.2
  56.4 11.5 %all_to_all.22.mixed_ref = bf16[8,32,256]{2,1,0:T(8,128)(2,1)S(1)} all-to-all(bf16[8,32,256]{2,1,0:T(8,128)(2,1)S(1)} %add_shards.1), channel_id=1, replica_groups={{5,4,3,2,1,0,7,6},{13,12,11,10,9,8,15,14},{21,20,19,18,17,16,23,22},{29..., dimensions={0} | all-to-all | bytes 262144 | tf_op jit(solution)/shard_map/all_to_all | solution.py:371
  67.9 0.0 copy-done
  67.9 0.0 copy-done.5
  67.9 1.1 %project.1 = (bf16[4,3,8,128]{3,2,1,0:T(8,128)(2,1)}, bf16[32,2048]{1,0:T(8,128)(2,1)}) custom-call(bf16[8,32,256]{2,1,0:T(8,128)(2,1)S(1)} %all_to_all.22.mixed_ref, bf16[16,128]{1,0:T(8,128)(2,1)S(1)} %bitcast.14, bf16[3,2048,128]{2,1,0:T(8,128)(2,1)S(1)} %bitcast.12), custom_call_target="tpu_custom_call" | custom-call | tf_op jit(solution)/shard_map/project/pallas_call | solution.py:372
  (1 shorter events, 0.0 us)
Async XLA Ops:
  2.1 23.0 %all-to-all-start = ((bf16[32,32,128]{2,1,0:T(8,128)(2,1)}), bf16[32,32,128]{2,1,0:T(8,128)(2,1)S(1)}, u32[]{:S(2)}, u32[]{:S(2)}) async-start(bf16[32,32,128]{2,1,0:T(8,128)(2,1)} %broadcast_in_dim.2), calls=%async_computation | async-start | bytes 524288 | tf_op jit(solution)/shard_map/all_to_all | solution.py:305
  17.7 26.5 %copy-start.1 = (bf16[128,2048]{1,0:T(8,128)(2,1)S(1)}, bf16[128,2048]{1,0:T(8,128)(2,1)}, u32[]{:S(2)}) copy-start(bf16[128,2048]{1,0:T(8,128)(2,1)} %weight_ref.1) | copy-start | bytes 1572868
  20.3 24.0 %copy-start.3 = (f32[40,128]{1,0:T(8,128)S(1)}, f32[40,128]{1,0:T(8,128)}, u32[]{:S(2)}) copy-start(f32[40,128]{1,0:T(8,128)} %get-tuple-element.8.level_ref) | copy-start | bytes 61444
  20.3 24.0 %copy-start.4 = (f32[32,128]{1,0:T(8,128)S(1)}, f32[32,128]{1,0:T(8,128)}, u32[]{:S(2)}) copy-start(f32[32,128]{1,0:T(8,128)} %get-tuple-element.7.mean_ref) | copy-start | bytes 49156
  22.8 33.6 %copy-start.2 = (bf16[4,8,2048]{2,1,0:T(8,128)(2,1)S(1)}, bf16[4,8,2048]{2,1,0:T(8,128)(2,1)}, u32[]{:S(2)}) copy-start(bf16[4,8,2048]{2,1,0:T(8,128)(2,1)} %param.16) | copy-start | bytes 393220
  25.9 42.0 %copy-start = (bf16[2048,3,128]{2,0,1:T(8,128)(2,1)S(1)}, bf16[2048,3,128]{2,0,1:T(8,128)(2,1)}, u32[]{:S(2)}) copy-start(bf16[2048,3,128]{2,0,1:T(8,128)(2,1)} %param.27) | copy-start | bytes 4718596
  25.9 42.0 %copy-start.5 = (bf16[2048]{0:T(1024)(128)(2,1)S(1)}, bf16[2048]{0:T(1024)(128)(2,1)}, u32[]{:S(2)}) copy-start(bf16[2048]{0:T(1024)(128)(2,1)} %param.26) | copy-start | bytes 12292

commit v7 on v6

--- a/solution.py
+++ b/solution.py
@@ -14,7 +14,7 @@
 NORM_EPS = 1e-05
 SCORE_SCALE = 1.0 / math.sqrt(HEAD_DIM)
 LANES = 2 * HEAD_DIM
-STAT_ROWS = 8
+STAT_ROWS = 2
 FIRST_CHIP = 21
 SHARD_ORDER = (5, 4, 3, 2, 1, 0, 7, 6)
 NOTE_ROWS = 16
@@ -94,9 +94,10 @@
         jnp.where(on_row, jnp.where(lane < HEAD_DIM, high, middle), 0.0), axis=0, keepdims=True
     )
     second = jnp.sum(jnp.where(on_row, low, 0.0), axis=0, keepdims=True)
-    stat_row = lax.broadcasted_iota(jnp.int32, (STAT_ROWS, LANES), 0)
-    stats = jnp.where(stat_row == 0, first, jnp.where(stat_row == 1, second, 0.0))
-    return jnp.concatenate([mean.astype(jnp.float32), stats], axis=0).astype(jnp.bfloat16)
+    mean = mean.astype(jnp.float32)
+    pieces = [mean[index : index + 2] for index in range(0, rows, 2)]
+    pieces.append(jnp.concatenate([first, second], axis=0))
+    return jnp.concatenate(pieces, axis=1).astype(jnp.bfloat16)
 
 
 def home_kernel(
@@ -215,6 +216,8 @@
     rows = mean_ref.shape[0]
     place = jnp.max(level_ref[rows:]).astype(jnp.int32)
     packet = result_ref[slot_of(place, result_ref.shape[0])].astype(jnp.float32)
+    pieces = [packet[:, index : index + LANES] for index in range(0, packet.shape[1], LANES)]
+    packet = jnp.concatenate(pieces, axis=0)
     wide = (2 * rows, LANES)
     lane = lax.broadcasted_iota(jnp.int32, wide, 1)
     row = lax.broadcasted_iota(jnp.int32, wide, 0)
@@ -342,7 +345,7 @@
     packet_rows = rows + STAT_ROWS
     results = pl.pallas_call(
         prompt_kernel,
-        out_shape=pltpu.VMEM((chips, packet_rows, lane_count), jnp.bfloat16),
+        out_shape=pltpu.VMEM((chips, 2, packet_rows // 2 * lane_count), jnp.bfloat16),
         in_specs=[VMEM_SPEC] * 2,
         out_specs=VMEM_SPEC,
         compiler_params=KERNEL_PARAMS,

time: 69.4 us -> 68.8 us (level)
  blocking collectives: 44 us -> 43.1 us
    all_to_all x1, blocking collectives: 18.3 us -> 17.4 us  [route(): return lax.all_to_all(slots, 'req', 0, 0, axis_index_groups=same_core)]
where the time goes in v7:
time: 68.8 us; the launch traced here: 68 us
  blocking collectives  43.1 us (63%)
  starting transfers between devices  13.7 us (20%)
  Pallas kernels  4.77 us (7%)
  between operations  2.68 us (4%)
  waiting for transfers between devices  2.29 us (3%)
  local copies, waits for them, and re-layouts  1.46 us (2%)
    all_to_all x1, blocking collectives, route(): return lax.all_to_all(slots, 'req', 0, 0, axis_index_groups=same_core)  17.4 us
    all_to_all x1, starting transfers between devices, route(): return lax.all_to_all(slots, 'req', 0, 0, axis_index_groups=same_core)  13.7 us
    all_to_all x1, blocking collectives, shards(): lax.all_to_all(partial, 'tp', 0, 0, axis_index_groups=shard_groups)  11.7 us
    all_to_all x1, blocking collectives, shards(): lax.all_to_all(mixed, 'tp', 0, 0, axis_index_groups=shard_groups)  11.5 us
    all_gather x1, blocking collectives, shards(): both_slots = lax.all_gather(own_slot, 'req', axis_index_groups=same_chip)  2.53 us
    pallas_call x1, Pallas kernels, shards(): pl.pallas_call(home_kernel, out_shape=(jax.ShapeDtypeStruct((rows, lane_c...  2.48 us
    all_to_all x1, waiting for transfers between devices, route(): return lax.all_to_all(slots, 'req', 0, 0, axis_index_groups=same_core)  2.29 us
    broadcast_in_dim x1, local copies, waits for them, and re-layouts, shards(): asked = route(jnp.broadcast_to(query_rows[None], (chips, rows, lane_count)))  1.43 us
  transfers between devices with their start and end apart: 1, of which 1 were waited for; matrix products, arithmetic and copies ran while one was open for 0% of the time, Pallas kernels for 4%

profile of v7, /device:TPU:6, one launch (start us, length us, event | category | flops | bytes accessed | tf_op | source)
XLA Modules:
  0.0 68.0 jit_solution(16442067887500411236)
XLA Ops:
  0.6 1.4 %broadcast_in_dim.2 = bf16[32,32,128]{2,1,0:T(8,128)(2,1)} broadcast(bf16[32,128]{1,0:T(8,128)(2,1)} %bitcast.17), dimensions={1,2} | broadcast | bytes 270336 | tf_op jit(solution)/shard_map/broadcast_in_dim | solution.py:311
  2.1 13.7 %all-to-all-start = ((bf16[32,32,128]{2,1,0:T(8,128)(2,1)}), bf16[32,32,128]{2,1,0:T(8,128)(2,1)S(1)}, u32[]{:S(2)}, u32[]{:S(2)}) async-start(bf16[32,32,128]{2,1,0:T(8,128)(2,1)} %broadcast_in_dim.2), calls=%async_computation | async-start | bytes 524288 | tf_op jit(solution)/shard_map/all_to_all | solution.py:308
  15.8 0.0 copy-start.1
  17.8 2.5 %home_attention.1 = (f32[32,128]{1,0:T(8,128)}, f32[40,128]{1,0:T(8,128)}, bf16[1040,128]{1,0:T(8,128)(2,1)}) custom-call(s32[1]{0:T(128)S(6)} %copy.17.owned_ref, s32[1]{0:T(128)S(6)} %copy.18.live_ref, s32[1]{0:T(128)S(6)} %copy.16.place_ref, s32[4,8]{1,0:T(4,128)} %bitcast.20, s32[8]{0:T(128)} %length_ref.1, s32[4,8]{1,0:T(4,128)} %parent_ref.1, ...), custom_call_target="tpu_custom_call" | custom-call | tf_op jit(solution)/shard_map/home_attention/pallas_call | solution.py:317
  20.3 0.0 copy-start.3
  20.3 0.0 copy-start.4
  20.3 2.5 %all-gather = bf16[2080,128]{1,0:T(8,128)(2,1)S(1)} all-gather(bf16[1040,128]{1,0:T(8,128)(2,1)} %get-tuple-element.9), channel_id=2, replica_groups={{0,8},{16,24},{32,40},{48,56},{64,72},{80,88},{96,104},{112,120},{128,1..., dimensions={0}, use_global_device_ids=true | all-gather | bytes 798720 | tf_op jit(solution)/shard_map/all_gather | solution.py:343
  22.8 0.0 copy-start.2
  22.8 2.3 %all-to-all-done.asked_ref = bf16[32,32,128]{2,1,0:T(8,128)(2,1)S(1)} async-done(((bf16[32,32,128]{2,1,0:T(8,128)(2,1)}), bf16[32,32,128]{2,1,0:T(8,128)(2,1)S(1)}, u32[]{:S(2)}, u32[]{:S(2)}) %all-to-all-start) | async-done | bytes 262176 | tf_op jit(solution)/shard_map/all_to_all | solution.py:308
  25.1 0.0 copy-start
  25.1 0.0 copy-start.5
  25.1 0.8 %prompt_attention.1 = bf16[32,2,2176]{2,1,0:T(2,128)(2,1)S(1)} custom-call(bf16[32,32,128]{2,1,0:T(8,128)(2,1)S(1)} %all-to-all-done.asked_ref, bf16[2,1040,128]{2,1,0:T(8,128)(2,1)S(1)} %bitcast.11), custom_call_target="tpu_custom_call" | custom-call | tf_op jit(solution)/shard_map/prompt_attention/pallas_call | solution.py:346
  25.9 17.4 %all_to_all.20.result_ref = bf16[32,2,2176]{2,1,0:T(2,128)(2,1)S(1)} all-to-all(bf16[32,2,2176]{2,1,0:T(2,128)(2,1)S(1)} %prompt_attention.1), channel_id=1, replica_groups={{336,352,368,384,400,416,432,448,464,480,496,0,16,32,48,64,80,96,112,12..., dimensions={0} | all-to-all | bytes 557056 | tf_op jit(solution)/shard_map/all_to_all | solution.py:308
  43.3 0.0 copy-done.1
  43.3 0.0 copy-done.3
  43.3 0.0 copy-done.4
  43.3 0.4 combine.1
  43.7 11.7 %all_to_all.21.partial_ref = bf16[8,32,256]{2,1,0:T(8,128)(2,1)S(1)} all-to-all(bf16[8,32,256]{2,1,0:T(8,128)(2,1)S(1)} %combine.1), channel_id=1, replica_groups={{5,4,3,2,1,0,7,6},{13,12,11,10,9,8,15,14},{21,20,19,18,17,16,23,22},{29..., dimensions={0} | all-to-all | bytes 262144 | tf_op jit(solution)/shard_map/all_to_all | solution.py:365
  55.4 0.0 copy-done.2
  55.4 11.5 %all_to_all.22.mixed_ref = bf16[8,32,256]{2,1,0:T(8,128)(2,1)S(1)} all-to-all(bf16[8,32,256]{2,1,0:T(8,128)(2,1)S(1)} %add_shards.1), channel_id=1, replica_groups={{5,4,3,2,1,0,7,6},{13,12,11,10,9,8,15,14},{21,20,19,18,17,16,23,22},{29..., dimensions={0} | all-to-all | bytes 262144 | tf_op jit(solution)/shard_map/all_to_all | solution.py:374
  66.9 0.0 copy-done
  66.9 0.0 copy-done.5
  66.9 1.1 %project.1 = (bf16[4,3,8,128]{3,2,1,0:T(8,128)(2,1)}, bf16[32,2048]{1,0:T(8,128)(2,1)}) custom-call(bf16[8,32,256]{2,1,0:T(8,128)(2,1)S(1)} %all_to_all.22.mixed_ref, bf16[16,128]{1,0:T(8,128)(2,1)S(1)} %bitcast.14, bf16[3,2048,128]{2,1,0:T(8,128)(2,1)S(1)} %bitcast.12), custom_call_target="tpu_custom_call" | custom-call | tf_op jit(solution)/shard_map/project/pallas_call | solution.py:375
  (1 shorter events, 0.0 us)
Async XLA Ops:
  2.1 23.0 %all-to-all-start = ((bf16[32,32,128]{2,1,0:T(8,128)(2,1)}), bf16[32,32,128]{2,1,0:T(8,128)(2,1)S(1)}, u32[]{:S(2)}, u32[]{:S(2)}) async-start(bf16[32,32,128]{2,1,0:T(8,128)(2,1)} %broadcast_in_dim.2), calls=%async_computation | async-start | bytes 524288 | tf_op jit(solution)/shard_map/all_to_all | solution.py:308
  15.8 27.5 %copy-start.1 = (bf16[128,2048]{1,0:T(8,128)(2,1)S(1)}, bf16[128,2048]{1,0:T(8,128)(2,1)}, u32[]{:S(2)}) copy-start(bf16[128,2048]{1,0:T(8,128)(2,1)} %weight_ref.1) | copy-start | bytes 1572868
  20.3 23.0 %copy-start.3 = (f32[40,128]{1,0:T(8,128)S(1)}, f32[40,128]{1,0:T(8,128)}, u32[]{:S(2)}) copy-start(f32[40,128]{1,0:T(8,128)} %get-tuple-element.8.level_ref) | copy-start | bytes 61444
  20.3 23.0 %copy-start.4 = (f32[32,128]{1,0:T(8,128)S(1)}, f32[32,128]{1,0:T(8,128)}, u32[]{:S(2)}) copy-start(f32[32,128]{1,0:T(8,128)} %get-tuple-element.7.mean_ref) | copy-start | bytes 49156
  22.8 32.6 %copy-start.2 = (bf16[4,8,2048]{2,1,0:T(8,128)(2,1)S(1)}, bf16[4,8,2048]{2,1,0:T(8,128)(2,1)}, u32[]{:S(2)}) copy-start(bf16[4,8,2048]{2,1,0:T(8,128)(2,1)} %param.16) | copy-start | bytes 393220
  25.1 41.8 %copy-start = (bf16[2048,3,128]{2,0,1:T(8,128)(2,1)S(1)}, bf16[2048,3,128]{2,0,1:T(8,128)(2,1)}, u32[]{:S(2)}) copy-start(bf16[2048,3,128]{2,0,1:T(8,128)(2,1)} %param.27) | copy-start | bytes 4718596
  25.1 41.8 %copy-start.5 = (bf16[2048]{0:T(1024)(128)(2,1)S(1)}, bf16[2048]{0:T(1024)(128)(2,1)}, u32[]{:S(2)}) copy-start(bf16[2048]{0:T(1024)(128)(2,1)} %param.26) | copy-start | bytes 12292

commit v8 on v7

--- a/solution.py
+++ b/solution.py
@@ -54,6 +54,7 @@
     tokens = slots_ref.shape[1] - NOTE_ROWS
     lane = lax.broadcasted_iota(jnp.int32, (NOTE_ROWS, LANES), 1)
     row = lax.broadcasted_iota(jnp.int32, (NOTE_ROWS, LANES), 0)
+    served = []
     for slot in range(2):
         note = slots_ref[slot, tokens:].astype(jnp.float32)
 
@@ -64,10 +65,14 @@
         owner = number(0)
         live = number(1) * 16 + number(2)
 
+        place = slot_of(owner, asked_ref.shape[0])
+        packet = prompt_packet(asked_ref[place], slots_ref[slot, :tokens], live, rows)
+        served.append((owner, place, packet))
+    for owner, place, packet in served:
+
         @pl.when(owner % 2 == core)
         def _():
-            place = slot_of(owner, asked_ref.shape[0])
-            out_ref[place] = prompt_packet(asked_ref[place], slots_ref[slot, :tokens], live, rows)
+            out_ref[place] = packet
 
 
 def prompt_packet(query_rows, cache, live, rows):

time: 68.8 us -> 68.7 us (level)
  no operation moved by 1% of the time
where the time goes in v8:
time: 68.7 us; the launch traced here: 68.2 us
  blocking collectives  43.1 us (63%)
  starting transfers between devices  13.7 us (20%)
  Pallas kernels  5.04 us (7%)
  between operations  2.68 us (4%)
  waiting for transfers between devices  2.29 us (3%)
  local copies, waits for them, and re-layouts  1.46 us (2%)
    all_to_all x1, blocking collectives, route(): return lax.all_to_all(slots, 'req', 0, 0, axis_index_groups=same_core)  17.3 us
    all_to_all x1, starting transfers between devices, route(): return lax.all_to_all(slots, 'req', 0, 0, axis_index_groups=same_core)  13.7 us
    all_to_all x1, blocking collectives, shards(): lax.all_to_all(partial, 'tp', 0, 0, axis_index_groups=shard_groups)  11.7 us
    all_to_all x1, blocking collectives, shards(): lax.all_to_all(mixed, 'tp', 0, 0, axis_index_groups=shard_groups)  11.5 us
    all_gather x1, blocking collectives, shards(): both_slots = lax.all_gather(own_slot, 'req', axis_index_groups=same_chip)  2.53 us
    pallas_call x1, Pallas kernels, shards(): pl.pallas_call(home_kernel, out_shape=(jax.ShapeDtypeStruct((rows, lane_c...  2.48 us
    all_to_all x1, waiting for transfers between devices, route(): return lax.all_to_all(slots, 'req', 0, 0, axis_index_groups=same_core)  2.29 us
    broadcast_in_dim x1, local copies, waits for them, and re-layouts, shards(): asked = route(jnp.broadcast_to(query_rows[None], (chips, rows, lane_count)))  1.43 us
  transfers between devices with their start and end apart: 1, of which 1 were waited for; matrix products, arithmetic and copies ran while one was open for 0% of the time, Pallas kernels for 4%

profile of v8, /device:TPU:6, one launch (start us, length us, event | category | flops | bytes accessed | tf_op | source)
XLA Modules:
  0.0 68.2 jit_solution(17601296907321010567)
XLA Ops:
  0.6 1.4 %broadcast_in_dim.2 = bf16[32,32,128]{2,1,0:T(8,128)(2,1)} broadcast(bf16[32,128]{1,0:T(8,128)(2,1)} %bitcast.17), dimensions={1,2} | broadcast | bytes 270336 | tf_op jit(solution)/shard_map/broadcast_in_dim | solution.py:316
  2.1 13.7 %all-to-all-start = ((bf16[32,32,128]{2,1,0:T(8,128)(2,1)}), bf16[32,32,128]{2,1,0:T(8,128)(2,1)S(1)}, u32[]{:S(2)}, u32[]{:S(2)}) async-start(bf16[32,32,128]{2,1,0:T(8,128)(2,1)} %broadcast_in_dim.2), calls=%async_computation | async-start | bytes 524288 | tf_op jit(solution)/shard_map/all_to_all | solution.py:313
  15.8 0.0 copy-start.1
  17.8 2.5 %home_attention.1 = (f32[32,128]{1,0:T(8,128)}, f32[40,128]{1,0:T(8,128)}, bf16[1040,128]{1,0:T(8,128)(2,1)}) custom-call(s32[1]{0:T(128)S(6)} %copy.17.owned_ref, s32[1]{0:T(128)S(6)} %copy.18.live_ref, s32[1]{0:T(128)S(6)} %copy.16.place_ref, s32[4,8]{1,0:T(4,128)} %bitcast.20, s32[8]{0:T(128)} %length_ref.1, s32[4,8]{1,0:T(4,128)} %parent_ref.1, ...), custom_call_target="tpu_custom_call" | custom-call | tf_op jit(solution)/shard_map/home_attention/pallas_call | solution.py:322
  20.3 0.0 copy-start.3
  20.3 0.0 copy-start.4
  20.3 2.5 %all-gather = bf16[2080,128]{1,0:T(8,128)(2,1)S(1)} all-gather(bf16[1040,128]{1,0:T(8,128)(2,1)} %get-tuple-element.9), channel_id=2, replica_groups={{0,8},{16,24},{32,40},{48,56},{64,72},{80,88},{96,104},{112,120},{128,1..., dimensions={0}, use_global_device_ids=true | all-gather | bytes 798720 | tf_op jit(solution)/shard_map/all_gather | solution.py:348
  22.8 0.0 copy-start.2
  22.8 2.3 %all-to-all-done.asked_ref = bf16[32,32,128]{2,1,0:T(8,128)(2,1)S(1)} async-done(((bf16[32,32,128]{2,1,0:T(8,128)(2,1)}), bf16[32,32,128]{2,1,0:T(8,128)(2,1)S(1)}, u32[]{:S(2)}, u32[]{:S(2)}) %all-to-all-start) | async-done | bytes 262176 | tf_op jit(solution)/shard_map/all_to_all | solution.py:313
  25.1 0.0 copy-start
  25.1 0.0 copy-start.5
  25.1 1.1 %prompt_attention.1 = bf16[32,2,2176]{2,1,0:T(2,128)(2,1)S(1)} custom-call(bf16[32,32,128]{2,1,0:T(8,128)(2,1)S(1)} %all-to-all-done.asked_ref, bf16[2,1040,128]{2,1,0:T(8,128)(2,1)S(1)} %bitcast.11), custom_call_target="tpu_custom_call" | custom-call | tf_op jit(solution)/shard_map/prompt_attention/pallas_call | solution.py:351
  26.2 17.3 %all_to_all.20.result_ref = bf16[32,2,2176]{2,1,0:T(2,128)(2,1)S(1)} all-to-all(bf16[32,2,2176]{2,1,0:T(2,128)(2,1)S(1)} %prompt_attention.1), channel_id=1, replica_groups={{336,352,368,384,400,416,432,448,464,480,496,0,16,32,48,64,80,96,112,12..., dimensions={0} | all-to-all | bytes 557056 | tf_op jit(solution)/shard_map/all_to_all | solution.py:313
  43.5 0.0 copy-done.1
  43.5 0.0 copy-done.3
  43.5 0.0 copy-done.4
  43.5 0.4 combine.1
  44.0 11.7 %all_to_all.21.partial_ref = bf16[8,32,256]{2,1,0:T(8,128)(2,1)S(1)} all-to-all(bf16[8,32,256]{2,1,0:T(8,128)(2,1)S(1)} %combine.1), channel_id=1, replica_groups={{5,4,3,2,1,0,7,6},{13,12,11,10,9,8,15,14},{21,20,19,18,17,16,23,22},{29..., dimensions={0} | all-to-all | bytes 262144 | tf_op jit(solution)/shard_map/all_to_all | solution.py:370
  55.7 0.0 copy-done.2
  55.7 11.5 %all_to_all.22.mixed_ref = bf16[8,32,256]{2,1,0:T(8,128)(2,1)S(1)} all-to-all(bf16[8,32,256]{2,1,0:T(8,128)(2,1)S(1)} %add_shards.1), channel_id=1, replica_groups={{5,4,3,2,1,0,7,6},{13,12,11,10,9,8,15,14},{21,20,19,18,17,16,23,22},{29..., dimensions={0} | all-to-all | bytes 262144 | tf_op jit(solution)/shard_map/all_to_all | solution.py:379
  67.2 0.0 copy-done
  67.2 0.0 copy-done.5
  67.2 1.1 %project.1 = (bf16[4,3,8,128]{3,2,1,0:T(8,128)(2,1)}, bf16[32,2048]{1,0:T(8,128)(2,1)}) custom-call(bf16[8,32,256]{2,1,0:T(8,128)(2,1)S(1)} %all_to_all.22.mixed_ref, bf16[16,128]{1,0:T(8,128)(2,1)S(1)} %bitcast.14, bf16[3,2048,128]{2,1,0:T(8,128)(2,1)S(1)} %bitcast.12), custom_call_target="tpu_custom_call" | custom-call | tf_op jit(solution)/shard_map/project/pallas_call | solution.py:380
  (1 shorter events, 0.0 us)
Async XLA Ops:
  2.1 23.0 %all-to-all-start = ((bf16[32,32,128]{2,1,0:T(8,128)(2,1)}), bf16[32,32,128]{2,1,0:T(8,128)(2,1)S(1)}, u32[]{:S(2)}, u32[]{:S(2)}) async-start(bf16[32,32,128]{2,1,0:T(8,128)(2,1)} %broadcast_in_dim.2), calls=%async_computation | async-start | bytes 524288 | tf_op jit(solution)/shard_map/all_to_all | solution.py:313
  15.8 27.7 %copy-start.1 = (bf16[128,2048]{1,0:T(8,128)(2,1)S(1)}, bf16[128,2048]{1,0:T(8,128)(2,1)}, u32[]{:S(2)}) copy-start(bf16[128,2048]{1,0:T(8,128)(2,1)} %weight_ref.1) | copy-start | bytes 1572868
  20.3 23.2 %copy-start.3 = (f32[40,128]{1,0:T(8,128)S(1)}, f32[40,128]{1,0:T(8,128)}, u32[]{:S(2)}) copy-start(f32[40,128]{1,0:T(8,128)} %get-tuple-element.8.level_ref) | copy-start | bytes 61444
  20.3 23.2 %copy-start.4 = (f32[32,128]{1,0:T(8,128)S(1)}, f32[32,128]{1,0:T(8,128)}, u32[]{:S(2)}) copy-start(f32[32,128]{1,0:T(8,128)} %get-tuple-element.7.mean_ref) | copy-start | bytes 49156
  22.8 32.9 %copy-start.2 = (bf16[4,8,2048]{2,1,0:T(8,128)(2,1)S(1)}, bf16[4,8,2048]{2,1,0:T(8,128)(2,1)}, u32[]{:S(2)}) copy-start(bf16[4,8,2048]{2,1,0:T(8,128)(2,1)} %param.16) | copy-start | bytes 393220
  25.1 42.1 %copy-start = (bf16[2048,3,128]{2,0,1:T(8,128)(2,1)S(1)}, bf16[2048,3,128]{2,0,1:T(8,128)(2,1)}, u32[]{:S(2)}) copy-start(bf16[2048,3,128]{2,0,1:T(8,128)(2,1)} %param.27) | copy-start | bytes 4718596
  25.1 42.1 %copy-start.5 = (bf16[2048]{0:T(1024)(128)(2,1)S(1)}, bf16[2048]{0:T(1024)(128)(2,1)}, u32[]{:S(2)}) copy-start(bf16[2048]{0:T(1024)(128)(2,1)} %param.26) | copy-start | bytes 12292
